TPU v7x, 256 devices: a whole 4x4x8 slice. The times are simulated.
256 devices in a mesh: row: 16 (over z, core), col: 16 (over x, y).
Axes of the slice: x: 4, y: 4, z: 8, core: 2. Of those that a mesh axis runs over, the one named last changes fastest.
Arguments:
- tokens: bfloat16 [4096, 8192], P('row', 'col'), may hold values from -6 to 6
- out_grad: bfloat16 [4096, 8192], P('row', 'col'), may hold values from -1.5 to 1.5
- gate_weight: bfloat16 [112, 1024, 128], P('col', 'row'), may hold values from -0.1875 to 0.1875
- up_weight: bfloat16 [112, 1024, 128], P('col', 'row'), may hold values from -0.1875 to 0.1875
- down_weight: bfloat16 [112, 1024, 128], P('col', 'row'), may hold values from -0.125 to 0.125
- gate_rows: int32 [112, 8], P('col'), may hold values from 0 to 63, all different within a row
- up_rows: int32 [112, 8], P('col'), may hold values from 0 to 63, all different within a row
- down_columns: int32 [112, 8], P('col'), may hold values from 0 to 63, all different within a row
Outputs:
- output: bfloat16 [4096, 8192], P('row', 'col')
- input_grad: bfloat16 [4096, 8192], P('row', 'col')
- gate_weight_grad: bfloat16 [112, 1024, 128], P('col', 'row')
- up_weight_grad: bfloat16 [112, 1024, 128], P('col', 'row')
- down_weight_grad: bfloat16 [112, 1024, 128], P('col', 'row')
Inputs may be any that keep to these rules, and one draw needn't show every extreme that they name: `gate_rows`: each row names 8 different block-rows; every block-row is named in some row. `up_rows`: each row names 8 different block-rows; every block-row is named in some row. `down_columns`: each row names 8 different output block-columns; every block-column is named in some row.
All inputs are finite; a program needn't handle non-finite values.
Results may differ from a plain program's by a relative error of at most 0.018.
Values may be sent and summed in bfloat16 or wider, within the bound.
A program may use at most 128 MiB of HBM per device.

v0:
```python
import jax
import jax.numpy as jnp
from jax import lax
from jax.sharding import PartitionSpec as P

D = 8192
BS = 128
KG = 8
KH = 8
DB = 64


def spread(contrib, block_lists):
    rows_here = contrib.shape[0]
    zero_block = jnp.zeros((rows_here, DB, BS), jnp.float32)
    placed = zero_block.at[:, block_lists.reshape(-1)].add(contrib.reshape(rows_here, -1, BS))
    return placed.reshape(rows_here, D)


def shards(tokens, out_grad, gate_weight, up_weight, down_weight, gate_rows, up_rows, down_columns):
    panel_in, panel_grad = (
        lax.all_gather(tokens, "col", axis=1, tiled=True),
        lax.all_gather(out_grad, "col", axis=1, tiled=True),
    )
    rows_here = panel_in.shape[0]
    gate_tiles, up_tiles, down_tiles = (
        lax.all_gather(gate_weight, "row", axis=1, tiled=True),
        lax.all_gather(up_weight, "row", axis=1, tiled=True),
        lax.all_gather(down_weight, "row", axis=1, tiled=True),
    )
    owned_slots = gate_tiles.shape[0]
    gate_four = gate_tiles.reshape(owned_slots, KG, BS, BS)
    up_four = up_tiles.reshape(owned_slots, KG, BS, BS)
    blocks_in = panel_in.reshape(rows_here, DB, BS)
    picked_gate = jnp.take(blocks_in, gate_rows.reshape(-1), axis=1).reshape(
        rows_here, owned_slots, KG, BS
    )
    picked_up = jnp.take(blocks_in, up_rows.reshape(-1), axis=1).reshape(
        rows_here, owned_slots, KG, BS
    )
    gate_value = jnp.einsum(
        "tfkr,fkri->tfi", picked_gate, gate_four, preferred_element_type=jnp.float32
    )
    up_value = jnp.einsum("tfkr,fkri->tfi", picked_up, up_four, preferred_element_type=jnp.float32)
    sigmoid_gate = jax.nn.sigmoid(gate_value)
    silu_gate = gate_value * sigmoid_gate
    hidden = (silu_gate * up_value).astype(jnp.bfloat16)
    down_four = down_tiles.reshape(owned_slots, KH, BS, BS)
    out_part = jnp.einsum("tfi,fkji->tfkj", hidden, down_four, preferred_element_type=jnp.float32)
    partial_out = spread(out_part, down_columns)
    out_sum = lax.psum_scatter(
        partial_out.astype(jnp.bfloat16), "col", scatter_dimension=1, tiled=True
    )
    blocks_grad = panel_grad.reshape(rows_here, DB, BS)
    picked_grad = jnp.take(blocks_grad, down_columns.reshape(-1), axis=1).reshape(
        rows_here, owned_slots, KH, BS
    )
    hidden_grad = jnp.einsum(
        "tfkj,fkji->tfi", picked_grad, down_four, preferred_element_type=jnp.float32
    )
    gate_grad = (
        hidden_grad * up_value * sigmoid_gate * (1.0 + gate_value * (1.0 - sigmoid_gate))
    ).astype(jnp.bfloat16)
    up_grad = (hidden_grad * silu_gate).astype(jnp.bfloat16)
    from_gate = jnp.einsum(
        "tfi,fkri->tfkr", gate_grad, gate_four, preferred_element_type=jnp.float32
    )
    from_up = jnp.einsum("tfi,fkri->tfkr", up_grad, up_four, preferred_element_type=jnp.float32)
    partial_in = spread(from_gate, gate_rows) + spread(from_up, up_rows)
    gate_partial = jnp.einsum(
        "tfkr,tfi->fkri", picked_gate, gate_grad, preferred_element_type=jnp.float32
    ).reshape(owned_slots, KG * BS, BS)
    up_partial = jnp.einsum(
        "tfkr,tfi->fkri", picked_up, up_grad, preferred_element_type=jnp.float32
    ).reshape(owned_slots, KG * BS, BS)
    down_partial = jnp.einsum(
        "tfkj,tfi->fkji", picked_grad, hidden, preferred_element_type=jnp.float32
    ).reshape(owned_slots, KH * BS, BS)
    gate_sum, up_sum, down_sum = (
        lax.psum_scatter(
            gate_partial.astype(jnp.bfloat16), "row", scatter_dimension=1, tiled=True
        ).astype(jnp.float32),
        lax.psum_scatter(
            up_partial.astype(jnp.bfloat16), "row", scatter_dimension=1, tiled=True
        ).astype(jnp.float32),
        lax.psum_scatter(
            down_partial.astype(jnp.bfloat16), "row", scatter_dimension=1, tiled=True
        ).astype(jnp.float32),
    )
    in_sum = lax.psum_scatter(
        partial_in.astype(jnp.bfloat16), "col", scatter_dimension=1, tiled=True
    )
    return (
        out_sum,
        in_sum,
        gate_sum.astype(jnp.bfloat16),
        up_sum.astype(jnp.bfloat16),
        down_sum.astype(jnp.bfloat16),
    )


def solution(mesh):
    in_specs = (
        P("row", "col"),
        P("row", "col"),
        P("col", "row", None),
        P("col", "row", None),
        P("col", "row", None),
        P("col", None),
        P("col", None),
        P("col", None),
    )
    out_specs = (
        P("row", "col"),
        P("row", "col"),
        P("col", "row", None),
        P("col", "row", None),
        P("col", "row", None),
    )
    return jax.shard_map(shards, mesh=mesh, in_specs=in_specs, out_specs=out_specs, check_vma=False)
```

profile of v0, /device:TPU:64, one launch (start us, length us, event | category | flops | bytes accessed | tf_op | source)
XLA Modules:
  0.0 644.7 jit_solution(5572205859742791919)
XLA Ops:
  7.2 1.8 copy.26
  9.1 1.8 copy.30
  10.9 0.7 all-gather.12.cloned.1.call-update
  12.3 0.5 all-gather.8.cloned.1.call-update
  12.8 0.8 reshape.164
  13.6 0.8 reshape.167
  14.4 0.8 reshape.174
  15.2 0.8 reshape.162
  16.0 53.8 %all-gather.6.cloned.1.call-done = bf16[256,8192]{0,1:T(8,128)(2,1)} async-done(((bf16[256,512]{0,1:T(8,128)(2,1)}), bf16[256,8192]{0,1:T(8,128)(2,1)}) %all-gather.6.cloned.1.call-update) | async-done | bytes 4194320 | tf_op jit(solution)/shard_map/all_gather | solution.py:22
  69.8 6.4 copy.27
  76.2 53.0 %all-gather.14.cloned.1.call-done = bf16[256,8192]{0,1:T(8,128)(2,1)} async-done(((bf16[256,512]{0,1:T(8,128)(2,1)}), bf16[256,8192]{0,1:T(8,128)(2,1)}) %all-gather.14.cloned.1.call-update) | async-done | bytes 4194320 | tf_op jit(solution)/shard_map/all_gather | solution.py:23
  129.1 6.4 copy.31
  135.6 5.1 gather_fusion.1
  140.6 5.1 gather_fusion
  145.8 5.1 gather_fusion.2
  150.8 4.4 broadcast_select_fusion
  155.2 2.3 broadcast_select_fusion.2
  157.5 1.1 copy-done
  158.6 2.3 broadcast_select_fusion.1
  160.9 7.7 %all-gather.12.cloned.1.call-done = bf16[7,1024,128]{2,1,0:T(8,128)(2,1)} async-done(((bf16[7,64,128]{2,1,0:T(8,128)(2,1)}), bf16[7,1024,128]{2,1,0:T(8,128)(2,1)}) %all-gather.12.cloned.1.call-update) | async-done | bytes 1835024 | tf_op jit(solution)/shard_map/all_gather | solution.py:29
  168.6 3.7 convolution_bitcast_fusion
  172.3 36.0 %all-gather.10.cloned.1.call-done = bf16[7,1024,128]{2,1,0:T(8,128)(2,1)} async-done(((bf16[7,64,128]{2,1,0:T(8,128)(2,1)}), bf16[7,1024,128]{2,1,0:T(8,128)(2,1)}) %all-gather.10.cloned.1.call-update) | async-done | bytes 1835024 | tf_op jit(solution)/shard_map/all_gather | solution.py:28
  208.3 4.7 convolution_bitcast_fusion.1
  213.0 35.1 %all-gather.8.cloned.1.call-done = bf16[7,1024,128]{2,1,0:T(8,128)(2,1)} async-done(((bf16[7,64,128]{2,1,0:T(8,128)(2,1)}), bf16[7,1024,128]{2,1,0:T(8,128)(2,1)}) %all-gather.8.cloned.1.call-update) | async-done | bytes 1835024 | tf_op jit(solution)/shard_map/all_gather | solution.py:27
  248.1 4.1 fusion.2
  252.2 4.1 fusion.9
  256.3 4.2 broadcast.57.clone
  260.6 19.0 %scatter_fusion = f32[256,64,128]{2,0,1:T(8,128)} fusion(f32[256,64,128]{2,0,1:T(8,128)} %broadcast.57.clone, s32[56]{0:T(128)S(1)} %fusion.6, f32[56,256,128]{2,1,0:T(8,128)} %bitcast.89), kind=kCustom, calls=%fused_computation.3 | custom fusion | flops 1835008 | bytes 22020320 | tf_op jit(solution)/shard_map/scatter-add | solution.py:16
  279.6 6.1 convert_element_type.46
  285.6 6.4 copy.29
  292.9 0.7 copy-done.3
  293.6 4.1 fusion.4
  297.7 4.2 broadcast.57.clone.1
  301.9 19.4 %scatter_fusion.1 = f32[256,64,128]{2,0,1:T(8,128)} fusion(f32[256,64,128]{2,0,1:T(8,128)} %broadcast.57.clone.1, s32[56]{0:T(128)S(1)} %fusion.7, f32[56,256,128]{2,1,0:T(8,128)} %bitcast.90), kind=kCustom, calls=%fused_computation.4 | custom fusion | flops 1835008 | bytes 22020320 | tf_op jit(solution)/shard_map/scatter-add | solution.py:16
  321.4 4.1 fusion.10
  325.5 4.3 broadcast.57.clone.2
  329.7 19.3 %scatter_fusion.2 = f32[256,64,128]{2,0,1:T(8,128)} fusion(f32[256,64,128]{2,0,1:T(8,128)} %broadcast.57.clone.2, s32[56]{0:T(128)S(1)} %fusion.8, f32[56,256,128]{2,1,0:T(8,128)} %bitcast.88), kind=kCustom, calls=%fused_computation.5 | custom fusion | flops 1835008 | bytes 22020320 | tf_op jit(solution)/shard_map/scatter-add | solution.py:16
  349.0 9.6 %add_convert_fusion = bf16[256,64,128]{2,0,1:T(8,128)(2,1)} fusion(f32[256,64,128]{2,0,1:T(8,128)} %scatter_fusion.1, f32[256,64,128]{2,0,1:T(8,128)} %scatter_fusion.2), kind=kLoop, calls=%fused_computation.6 | loop fusion | flops 4194304 | bytes 20971520 | tf_op jit(solution)/shard_map/convert_element_type | solution.py:91
  358.6 6.4 copy.32
  365.1 4.7 convolution_convert_fusion
  369.8 4.6 convolution_convert_fusion.2
  374.5 4.7 convolution_convert_fusion.1
  379.3 1.8 copy.36
  381.1 80.1 %reduce-scatter.8.cloned.1.call-done = bf16[256,512]{0,1:T(8,128)(2,1)} async-done(((bf16[256,8192]{0,1:T(8,128)(2,1)}), bf16[256,512]{0,1:T(8,128)(2,1)}) %reduce-scatter.8.cloned.1.call-update) | async-done | bytes 262160 | tf_op jit(solution)/shard_map/reduce_scatter | solution.py:90
  461.2 1.8 copy.37
  463.0 54.0 %reduce-scatter.14.cloned.1.call-done = bf16[7,64,128]{2,1,0:T(8,128)(2,1)} async-done(((bf16[7,1024,128]{2,1,0:T(8,128)(2,1)}), bf16[7,64,128]{2,1,0:T(8,128)(2,1)}) %reduce-scatter.14.cloned.1.call-update) | async-done | bytes 114704 | tf_op jit(solution)/shard_map/reduce_scatter | solution.py:86
  517.0 60.6 %reduce-scatter.10.cloned.1.call-done = bf16[7,64,128]{2,1,0:T(8,128)(2,1)} async-done(((bf16[7,1024,128]{2,1,0:T(8,128)(2,1)}), bf16[7,64,128]{2,1,0:T(8,128)(2,1)}) %reduce-scatter.10.cloned.1.call-update) | async-done | bytes 114704 | tf_op jit(solution)/shard_map/reduce_scatter | solution.py:80
  577.6 60.3 %reduce-scatter.12.cloned.1.call-done = bf16[7,64,128]{2,1,0:T(8,128)(2,1)} async-done(((bf16[7,1024,128]{2,1,0:T(8,128)(2,1)}), bf16[7,64,128]{2,1,0:T(8,128)(2,1)}) %reduce-scatter.12.cloned.1.call-update) | async-done | bytes 114704 | tf_op jit(solution)/shard_map/reduce_scatter | solution.py:83
  (45 shorter events, 1.9 us)
Async XLA Ops:
  7.2 62.7 %all-gather.6.cloned.1.call-start = ((), (), s32[]{:S(2)}) async-start(), calls=%async_computation.5 | async-start | bytes 4456448 | tf_op jit(solution)/shard_map/all_gather | solution.py:22
  9.0 120.1 %all-gather.14.cloned.1.call-start = ((), (), s32[]{:S(2)}) async-start(), calls=%async_computation.10 | async-start | bytes 4456448 | tf_op jit(solution)/shard_map/all_gather | solution.py:23
  10.9 157.7 %all-gather.12.cloned.1.call-start = ((), (), s32[]{:S(2)}) async-start(), calls=%async_computation.8 | async-start | bytes 1949696 | tf_op jit(solution)/shard_map/all_gather | solution.py:29
  11.6 196.7 %all-gather.10.cloned.1.call-start = ((), (), s32[]{:S(2)}) async-start(), calls=%async_computation.7 | async-start | bytes 1949696 | tf_op jit(solution)/shard_map/all_gather | solution.py:28
  12.2 235.9 %all-gather.8.cloned.1.call-start = ((), (), s32[]{:S(2)}) async-start(), calls=%async_computation.6 | async-start | bytes 1949696 | tf_op jit(solution)/shard_map/all_gather | solution.py:27
  12.8 366.5 %reduce-scatter.6.cloned.1.call-start = ((), (), s32[]{:S(2)}) async-start(), calls=%async_computation.9 | async-start | bytes 4456448 | tf_op jit(solution)/shard_map/reduce_scatter | solution.py:51
  150.8 4.4 copy-start.1
  155.2 3.4 copy-start
  248.1 4.1 copy-start.4
  292.0 0.7 copy-start.5
  292.0 0.8 copy-start.6
  292.0 1.5 copy-start.3
  292.1 169.1 %reduce-scatter.8.cloned.1.call-start = ((), (), s32[]{:S(2)}) async-start(), calls=%async_computation.11 | async-start | bytes 4456448 | tf_op jit(solution)/shard_map/reduce_scatter | solution.py:90
  301.9 19.5 %copy-start.2 = (bf16[7,1024,128]{2,1,0:T(8,128)(2,1)S(1)}, bf16[7,1024,128]{2,1,0:T(8,128)(2,1)}, u32[]{:S(2)}) copy-start(bf16[7,1024,128]{2,1,0:T(8,128)(2,1)} %all-gather.10.cloned.1.call-done) | copy-start | bytes 5505028
  365.0 152.0 %reduce-scatter.14.cloned.1.call-start = ((), (), s32[]{:S(2)}) async-start(), calls=%async_computation.14 | async-start | bytes 1949696 | tf_op jit(solution)/shard_map/reduce_scatter | solution.py:86
  369.7 207.8 %reduce-scatter.10.cloned.1.call-start = ((), (), s32[]{:S(2)}) async-start(), calls=%async_computation.12 | async-start | bytes 1949696 | tf_op jit(solution)/shard_map/reduce_scatter | solution.py:80
  374.4 263.4 %reduce-scatter.12.cloned.1.call-start = ((), (), s32[]{:S(2)}) async-start(), calls=%async_computation.13 | async-start | bytes 1949696 | tf_op jit(solution)/shard_map/reduce_scatter | solution.py:83
Sparse Core Ops, SparseCore 0:
  11.0 58.7 all-gather.5
  72.8 56.2 all-gather.13
  131.0 37.5 all-gather.11
  170.3 37.9 all-gather.9
  210.0 37.9 all-gather.7
  292.2 82.8 reduce-scatter.5
  379.1 82.0 reduce-scatter.7
  464.3 52.6 reduce-scatter.13
  520.3 57.2 reduce-scatter.9
  580.5 57.2 reduce-scatter.11
where the time goes:
time: 652 us; the launch traced here: 645 us
  waiting for transfers between devices  442 us (68%)
  other arithmetic  82.4 us (13%)
  local copies, waits for them, and re-layouts  66.2 us (10%)
  matrix products  38.8 us (6%)
  between operations  14.3 us (2%)
    reduce_scatter x1, waiting for transfers between devices, shards(): lax.psum_scatter(partial_in.astype(jnp.bfloat16), 'col', scatter_dimensio...  80.1 us
    reduce_scatter x1, waiting for transfers between devices, shards(): lax.psum_scatter(gate_partial.astype(jnp.bfloat16), 'row', scatter_dimens...  60.6 us
    reduce_scatter x1, waiting for transfers between devices, shards(): lax.psum_scatter(up_partial.astype(jnp.bfloat16), 'row', scatter_dimensio...  60.3 us
    scatter-add x3, other arithmetic, spread(): zero_block.at[:, block_lists.reshape(-1)]  57.7 us
    reduce_scatter x1, waiting for transfers between devices, shards(): lax.psum_scatter(down_partial.astype(jnp.bfloat16), 'row', scatter_dimens...  54 us
    all_gather x1, waiting for transfers between devices, shards(): lax.all_gather(tokens, 'col', axis=1, tiled=True)  53.8 us
    all_gather x1, waiting for transfers between devices, shards(): lax.all_gather(out_grad, 'col', axis=1, tiled=True)  53 us
    all_gather x1, waiting for transfers between devices, shards(): lax.all_gather(up_weight, 'row', axis=1, tiled=True)  36 us
  transfers between devices with their start and end apart: 10, of which 9 were waited for; matrix products, arithmetic and copies ran while one was open for 22% of the time, Pallas kernels for 0%

commit v1 on v0

--- a/solution.py
+++ b/solution.py
@@ -18,17 +18,16 @@
 
 
 def shards(tokens, out_grad, gate_weight, up_weight, down_weight, gate_rows, up_rows, down_columns):
-    panel_in, panel_grad = (
-        lax.all_gather(tokens, "col", axis=1, tiled=True),
-        lax.all_gather(out_grad, "col", axis=1, tiled=True),
+    panels = lax.all_gather(jnp.stack([tokens, out_grad]), "col", axis=2, tiled=True)
+    panel_in, panel_grad = panels[0], panels[1]
+    rows_here = panel_in.shape[0]
+    owned_slots = gate_weight.shape[0]
+    tiles = lax.all_gather(
+        jnp.concatenate([gate_weight, up_weight, down_weight], axis=0), "row", axis=1, tiled=True
     )
-    rows_here = panel_in.shape[0]
-    gate_tiles, up_tiles, down_tiles = (
-        lax.all_gather(gate_weight, "row", axis=1, tiled=True),
-        lax.all_gather(up_weight, "row", axis=1, tiled=True),
-        lax.all_gather(down_weight, "row", axis=1, tiled=True),
-    )
-    owned_slots = gate_tiles.shape[0]
+    gate_tiles = tiles[:owned_slots]
+    up_tiles = tiles[owned_slots : 2 * owned_slots]
+    down_tiles = tiles[2 * owned_slots :]
     gate_four = gate_tiles.reshape(owned_slots, KG, BS, BS)
     up_four = up_tiles.reshape(owned_slots, KG, BS, BS)
     blocks_in = panel_in.reshape(rows_here, DB, BS)
@@ -48,9 +47,6 @@
     down_four = down_tiles.reshape(owned_slots, KH, BS, BS)
     out_part = jnp.einsum("tfi,fkji->tfkj", hidden, down_four, preferred_element_type=jnp.float32)
     partial_out = spread(out_part, down_columns)
-    out_sum = lax.psum_scatter(
-        partial_out.astype(jnp.bfloat16), "col", scatter_dimension=1, tiled=True
-    )
     blocks_grad = panel_grad.reshape(rows_here, DB, BS)
     picked_grad = jnp.take(blocks_grad, down_columns.reshape(-1), axis=1).reshape(
         rows_here, owned_slots, KH, BS
@@ -76,26 +72,24 @@
     down_partial = jnp.einsum(
         "tfkj,tfi->fkji", picked_grad, hidden, preferred_element_type=jnp.float32
     ).reshape(owned_slots, KH * BS, BS)
-    gate_sum, up_sum, down_sum = (
-        lax.psum_scatter(
-            gate_partial.astype(jnp.bfloat16), "row", scatter_dimension=1, tiled=True
-        ).astype(jnp.float32),
-        lax.psum_scatter(
-            up_partial.astype(jnp.bfloat16), "row", scatter_dimension=1, tiled=True
-        ).astype(jnp.float32),
-        lax.psum_scatter(
-            down_partial.astype(jnp.bfloat16), "row", scatter_dimension=1, tiled=True
-        ).astype(jnp.float32),
+    tile_sums = lax.psum_scatter(
+        jnp.concatenate([gate_partial, up_partial, down_partial], axis=0).astype(jnp.bfloat16),
+        "row",
+        scatter_dimension=1,
+        tiled=True,
     )
-    in_sum = lax.psum_scatter(
-        partial_in.astype(jnp.bfloat16), "col", scatter_dimension=1, tiled=True
+    panel_sums = lax.psum_scatter(
+        jnp.stack([partial_out, partial_in]).astype(jnp.bfloat16),
+        "col",
+        scatter_dimension=2,
+        tiled=True,
     )
     return (
-        out_sum,
-        in_sum,
-        gate_sum.astype(jnp.bfloat16),
-        up_sum.astype(jnp.bfloat16),
-        down_sum.astype(jnp.bfloat16),
+        panel_sums[0],
+        panel_sums[1],
+        tile_sums[:owned_slots],
+        tile_sums[owned_slots : 2 * owned_slots],
+        tile_sums[2 * owned_slots :],
     )
 
 

time: 652 us -> 437 us (0.67)
  waiting for transfers between devices: 442 us -> 203 us
  local copies, waits for them, and re-layouts: 66.2 us -> 102 us
  matrix products: 38.8 us -> 24.6 us
  other arithmetic: 82.4 us -> 91 us
    reduce_scatter x5 -> x2, waiting for transfers between devices: 255 us -> 88.1 us  [the longest x1 88.1 us: shards(): lax.psum_scatter(jnp.stack([partial_out, partial_in]).astype(jnp.bfloat16...]
    all_gather x5 -> x2, waiting for transfers between devices: 186 us -> 115 us  [the longest x1 72.9 us: shards(): lax.all_gather(jnp.stack([tokens, out_grad]), 'col', axis=2, tiled=True)]
    another operation x3 -> x7, local copies, waits for them, and re-layouts: 12.8 us -> 38.3 us
    another operation x0 -> x4, other arithmetic: none -> 23.9 us
    convert_element_type x2 -> x0, other arithmetic: 15.7 us -> none  [the longest x1 9.62 us: shards(): partial_in.astype(jnp.bfloat16)]
    convert_element_type x2 -> x0, local copies, waits for them, and re-layouts: 12.8 us -> none  [the longest x1 6.4 us: shards(): partial_out.astype(jnp.bfloat16)]
    reshape x2 -> x3, local copies, waits for them, and re-layouts: 12.8 us -> 25.1 us  [spread(): contrib.reshape(rows_here, -1, BS)]
    slice x0 -> x3, local copies, waits for them, and re-layouts: none -> 12.3 us  [the longest x1 5.71 us: shards(): panel_in, panel_grad = (panels[0], panels[1])]
  transfers between devices with their start and end apart: 10 -> 4, of which waited for: 9 -> 3; matrix products, arithmetic and copies ran while one was open for 22% -> 36% of each run, Pallas kernels for 0% -> 0%
where the time goes in v1:
time: 437 us; the launch traced here: 435 us
  waiting for transfers between devices  203 us (46%)
  local copies, waits for them, and re-layouts  102 us (23%)
  other arithmetic  91 us (21%)
  matrix products  24.6 us (6%)
  between operations  14 us (3%)
    reduce_scatter x1, waiting for transfers between devices, shards(): lax.psum_scatter(jnp.stack([partial_out, partial_in]).astype(jnp.bfloat16...  88.1 us
    all_gather x1, waiting for transfers between devices, shards(): lax.all_gather(jnp.stack([tokens, out_grad]), 'col', axis=2, tiled=True)  72.9 us
    scatter-add x3, other arithmetic, spread(): zero_block.at[:, block_lists.reshape(-1)]  56.9 us
    all_gather x1, waiting for transfers between devices, shards(): lax.all_gather(jnp.concatenate([gate_weight, up_weight, down_weight], axi...  42 us
    another operation x5, local copies, waits for them, and re-layouts  25.5 us
    reshape x3, local copies, waits for them, and re-layouts, spread(): contrib.reshape(rows_here, -1, BS)  25.1 us
    another operation x2, other arithmetic  15.6 us
  transfers between devices with their start and end apart: 4, of which 3 were waited for; matrix products, arithmetic and copies ran while one was open for 36% of the time, Pallas kernels for 0%

profile of v1, /device:TPU:64, one launch (start us, length us, event | category | flops | bytes accessed | tf_op | source)
XLA Modules:
  0.0 435.0 jit_solution(9459463797062491396)
XLA Ops:
  7.2 1.8 pad_maximum_fusion.3
  9.1 1.1 copy.50
  10.2 1.1 copy.51
  11.3 0.8 pad_maximum_fusion.2
  12.2 0.8 reshape.183
  13.2 42.0 %all-gather.3.cloned.1.call-done = bf16[21,1024,128]{2,1,0:T(8,128)(2,1)} async-done(((bf16[21,64,128]{2,1,0:T(8,128)(2,1)}), bf16[21,1024,128]{2,1,0:T(8,128)(2,1)}) %all-gather.3.cloned.1.call-update) | async-done | bytes 5505040 | tf_op jit(solution)/shard_map/all_gather | solution.py:25
  55.2 4.9 %fusion.10 = (bf16[7,1024,128]{2,1,0:T(8,128)(2,1)}, bf16[7,1024,128]{2,1,0:T(8,128)(2,1)}, bf16[7,1024,128]{2,1,0:T(8,128)(2,1)S(1)}) fusion(bf16[21,1024,128]{2,1,0:T(8,128)(2,1)} %all-gather.3.cloned.1.call-done), kind=kLoop, calls=%fused_computation.48 | loop fusion | bytes 11010048 | tf_op jit(solution)/shard_map/slice | solution.py:29
  60.1 72.9 %all-gather.5.cloned.1.call-done = bf16[2,256,8192]{1,2,0:T(8,128)(2,1)} async-done(((bf16[2,256,512]{1,2,0:T(8,128)(2,1)}), bf16[2,256,8192]{1,2,0:T(8,128)(2,1)}) %all-gather.5.cloned.1.call-update) | async-done | bytes 8388624 | tf_op jit(solution)/shard_map/all_gather | solution.py:21
  133.0 5.7 %fusion.9 = (bf16[1,256,8192]{1,2,0:T(8,128)(2,1)}, bf16[1,256,8192]{1,2,0:T(8,128)(2,1)}) fusion(bf16[2,256,8192]{1,2,0:T(8,128)(2,1)} %all-gather.5.cloned.1.call-done), kind=kLoop, calls=%fused_computation.47 | loop fusion | bytes 16777216 | tf_op jit(solution)/shard_map/slice | solution.py:22
  138.7 6.4 %copy.52 = bf16[256,64,128]{2,0,1:T(8,128)(2,1)} copy(bf16[256,64,128]{0,2,1:T(8,128)(2,1)} %bitcast.106) | data formatting | bytes 8388608 | tf_op jit(solution)/shard_map/reshape;squeeze | solution.py:33
  145.2 6.4 %copy.59 = bf16[256,64,128]{2,0,1:T(8,128)(2,1)} copy(bf16[256,64,128]{0,2,1:T(8,128)(2,1)} %bitcast.105) | data formatting | bytes 8388608 | tf_op jit(solution)/shard_map/reshape;squeeze | solution.py:50
  151.5 5.1 %gather_fusion.1 = bf16[56,256,128]{2,1,0:T(8,128)(2,1)} fusion(bf16[256,64,128]{2,0,1:T(8,128)(2,1)} %copy.52, s32[1024]{0:T(1024)S(1)} %pad_clamp_fusion.1), kind=kCustom, calls=%fused_computation.1.clone | custom fusion | bytes 7340256 | tf_op jit(solution)/shard_map/jit(_take)/gather | solution.py:37
  156.6 5.1 %gather_fusion = bf16[56,256,128]{2,1,0:T(8,128)(2,1)} fusion(bf16[256,64,128]{2,0,1:T(8,128)(2,1)} %copy.52, s32[1024]{0:T(1024)S(1)} %pad_clamp_fusion.2), kind=kCustom, calls=%fused_computation.clone | custom fusion | bytes 7340256 | tf_op jit(solution)/shard_map/jit(_take)/gather | solution.py:34
  161.7 2.6 broadcast_select_fusion.1
  164.2 1.8 copy-done
  166.0 2.3 convolution_bitcast_fusion.1
  168.3 5.1 %gather_fusion.2 = bf16[56,256,128]{2,1,0:T(8,128)(2,1)} fusion(bf16[256,64,128]{2,0,1:T(8,128)(2,1)} %copy.59, s32[1024]{0:T(1024)S(1)} %pad_clamp_fusion), kind=kCustom, calls=%fused_computation.2.clone | custom fusion | bytes 7340256 | tf_op jit(solution)/shard_map/jit(_take)/gather | solution.py:51
  173.4 2.4 broadcast_select_fusion
  175.9 1.4 convolution_bitcast_fusion
  177.2 0.7 copy-done.3
  178.3 1.1 copy-done.4
  179.6 1.6 fusion.1
  181.2 1.4 convolution_convert_fusion.2
  183.2 1.4 convolution_convert_fusion.1
  184.6 1.4 convolution_convert_fusion
  186.0 2.9 pad_maximum_fusion.1
  189.9 5.6 %fusion.13 = f32[7,8,128,256]{3,2,1,0:T(8,128)} fusion(bf16[7,8,128,128]{3,2,1,0:T(8,128)(2,1)} %bitcast.110, bf16[256,7,128,1]{0,2,3,1:T(8,128)(2,1)S(1)} %get-tuple-element.23), kind=kOutput, calls=%fused_computation.51 | convolution fusion | flops 469762048 | bytes 9633792 | tf_op jit(solution)/shard_map/tfi,fkri->tfkr/dot_general | solution.py:64
  195.5 8.4 %copy.64 = f32[256,56,128]{2,0,1:T(8,128)} copy(f32[256,56,128]{0,2,1:T(8,128)} %bitcast.98) | data formatting | bytes 14680064 | tf_op jit(solution)/shard_map/reshape | solution.py:16
  203.8 5.6 %fusion.4 = f32[7,8,128,256]{3,2,1,0:T(8,128)} fusion(bf16[7,8,128,128]{3,2,1,0:T(8,128)(2,1)} %bitcast.114, bf16[256,7,128]{0,2,1:T(8,128)(2,1)S(1)} %get-tuple-element.22), kind=kOutput, calls=%fused_computation.27 | convolution fusion | flops 469762048 | bytes 9633792 | tf_op jit(solution)/shard_map/tfi,fkri->tfkr/dot_general | solution.py:61
  209.5 8.4 %copy.62 = f32[256,56,128]{2,0,1:T(8,128)} copy(f32[256,56,128]{0,2,1:T(8,128)} %bitcast.99) | data formatting | bytes 14680064 | tf_op jit(solution)/shard_map/reshape | solution.py:16
  217.9 4.3 broadcast.57.clone.1
  222.1 19.0 %scatter_fusion.2 = f32[256,64,128]{2,0,1:T(8,128)} fusion(f32[256,64,128]{2,0,1:T(8,128)} %broadcast.57.clone.1, s32[56]{0:T(128)S(1)} %fusion.8, f32[56,256,128]{2,1,0:T(8,128)} %bitcast.101), kind=kCustom, calls=%fused_computation.5 | custom fusion | flops 1835008 | bytes 22020320 | tf_op jit(solution)/shard_map/scatter-add | solution.py:16
  241.2 4.2 broadcast.57.clone
  245.4 18.9 %scatter_fusion.1 = f32[256,64,128]{2,0,1:T(8,128)} fusion(f32[256,64,128]{2,0,1:T(8,128)} %broadcast.57.clone, s32[56]{0:T(128)S(1)} %fusion.7, f32[56,256,128]{2,1,0:T(8,128)} %bitcast.102), kind=kCustom, calls=%fused_computation.4 | custom fusion | flops 1835008 | bytes 22020320 | tf_op jit(solution)/shard_map/scatter-add | solution.py:16
  264.4 9.5 %add_convert_fusion = bf16[256,64,128]{2,0,1:T(8,128)(2,1)} fusion(f32[256,64,128]{2,0,1:T(8,128)} %scatter_fusion.1, f32[256,64,128]{2,0,1:T(8,128)} %scatter_fusion.2), kind=kLoop, calls=%fused_computation.7 | loop fusion | flops 4194304 | bytes 20971520 | tf_op jit(solution)/shard_map/convert.8
  273.9 6.4 %copy.65 = bf16[256,64,128]{0,2,1:T(8,128)(2,1)} copy(bf16[256,64,128]{2,0,1:T(8,128)(2,1)} %add_convert_fusion) | data formatting | bytes 8388608 | tf_op jit(solution)/shard_map/convert.8
  280.3 4.0 fusion.12
  284.3 8.3 %copy.57 = f32[256,56,128]{2,0,1:T(8,128)} copy(f32[256,56,128]{0,2,1:T(8,128)} %bitcast.100) | data formatting | bytes 14680064 | tf_op jit(solution)/shard_map/reshape | solution.py:16
  292.7 4.2 broadcast.57.clone.2
  296.9 19.0 %scatter_fusion = f32[256,64,128]{2,0,1:T(8,128)} fusion(f32[256,64,128]{2,0,1:T(8,128)} %broadcast.57.clone.2, s32[56]{0:T(128)S(1)} %fusion.6, f32[56,256,128]{2,1,0:T(8,128)} %bitcast.103), kind=kCustom, calls=%fused_computation.3 | custom fusion | flops 1835008 | bytes 22020320 | tf_op jit(solution)/shard_map/scatter-add | solution.py:16
  315.9 6.1 %convert.20 = bf16[256,64,128]{2,0,1:T(8,128)(2,1)} convert(f32[256,64,128]{2,0,1:T(8,128)} %scatter_fusion) | non-fusion elementwise | flops 2097152 | bytes 12582912 | tf_op jit(solution)/shard_map/convert.9
  321.9 6.4 %copy.58 = bf16[256,64,128]{0,2,1:T(8,128)(2,1)} copy(bf16[256,64,128]{2,0,1:T(8,128)(2,1)} %convert.20) | data formatting | bytes 8388608 | tf_op jit(solution)/shard_map/convert.9
  328.3 7.4 %pad_maximum_fusion = bf16[2,256,8192]{1,2,0:T(8,128)(2,1)} fusion(bf16[1,256,8192]{1,2,0:T(8,128)(2,1)} %bitcast.104, bf16[1,256,8192]{1,2,0:T(8,128)(2,1)} %bitcast.107), kind=kLoop, calls=%fused_computation.6 | loop fusion | flops 4194304 | bytes 16777216 | tf_op jit(solution)/shard_map/stack | solution.py:82
  335.8 1.7 fusion.11
  337.6 88.1 %reduce-scatter.3.cloned.1.call-done = bf16[2,256,512]{1,2,0:T(8,128)(2,1)} async-done(((bf16[2,256,8192]{1,2,0:T(8,128)(2,1)}), bf16[2,256,512]{1,2,0:T(8,128)(2,1)}) %reduce-scatter.3.cloned.1.call-update) | async-done | bytes 524304 | tf_op jit(solution)/shard_map/reduce_scatter | solution.py:81
  425.7 1.1 slice_bitcast_fusion
  426.7 0.8 copy.72
  427.6 0.8 copy.73
  (42 shorter events, 2.6 us)
Async XLA Ops:
  7.2 5.8 %copy-start.8 = (s32[7,8]{1,0:T(8,128)S(1)}, s32[7,8]{1,0:T(8,128)}, u32[]{:S(2)}) copy-start(s32[7,8]{1,0:T(8,128)} %param.17) | copy-start | bytes 676
  7.2 5.9 %copy-start.7 = (s32[7,8]{1,0:T(8,128)S(1)}, s32[7,8]{1,0:T(8,128)}, u32[]{:S(2)}) copy-start(s32[7,8]{1,0:T(8,128)} %param.15) | copy-start | bytes 676
  7.2 48.1 %all-gather.3.cloned.1.call-start = ((), (), s32[]{:S(2)}) async-start(), calls=%async_computation.2 | async-start | bytes 5849088 | tf_op jit(solution)/shard_map/all_gather | solution.py:25
  9.0 124.0 %all-gather.5.cloned.1.call-start = ((), (), s32[]{:S(2)}) async-start(), calls=%async_computation.3 | async-start | bytes 8912896 | tf_op jit(solution)/shard_map/all_gather | solution.py:21
  12.1 323.7 %reduce-scatter.5.cloned.1.call-start = ((), (), s32[]{:S(2)}) async-start(), calls=%async_computation.5 | async-start | bytes 5849088 | tf_op jit(solution)/shard_map/reduce_scatter | solution.py:75
  161.7 4.4 %copy-start.2 = (bf16[7,1024,128]{2,1,0:T(8,128)(2,1)S(1)}, bf16[7,1024,128]{2,1,0:T(8,128)(2,1)}, u32[]{:S(2)}) copy-start(bf16[7,1024,128]{2,1,0:T(8,128)(2,1)} %get-tuple-element.18) | copy-start | bytes 5505028
  164.2 1.8 copy-start
  175.8 2.0 copy-start.3
  177.9 1.5 copy-start.4
  177.9 1.7 copy-start.5
  181.2 2.0 copy-start.1
  188.9 0.7 copy-start.6
  188.9 236.7 %reduce-scatter.3.cloned.1.call-start = ((), (), s32[]{:S(2)}) async-start(), calls=%async_computation.4 | async-start | bytes 8912896 | tf_op jit(solution)/shard_map/reduce_scatter | solution.py:81
Sparse Core Ops, SparseCore 0:
  9.9 45.3 all-gather.2
  57.7 75.2 all-gather.4
  189.1 59.1 reduce-scatter.4
  335.9 89.7 reduce-scatter.2

commit v2 on v1

v2 whole, which is shorter than its diff:
```python
import functools

import jax
import jax.numpy as jnp
from jax import lax
from jax.experimental import pallas as pl
from jax.experimental.pallas import tpu as pltpu
from jax.sharding import PartitionSpec as P

BS = 128
KG = 8
KH = 8


def core_kernel(slots, gr_ref, ur_ref, dc_ref, p_ref, w_ref, panel_ref, tiles_ref, out_acc, in_acc):
    out_acc[...] = jnp.zeros_like(out_acc)
    in_acc[...] = jnp.zeros_like(in_acc)
    f32 = jnp.float32
    bf16 = jnp.bfloat16
    rows = p_ref.shape[1]
    tn = (((0,), (0,)), ((), ()))
    nt = (((1,), (1,)), ((), ()))

    def col(b):
        return pl.ds(pl.multiple_of(b * BS, BS), BS)

    def body(f, carry):
        gate = jnp.zeros((rows, BS), f32)
        up = jnp.zeros((rows, BS), f32)
        hg = jnp.zeros((rows, BS), f32)
        for k in range(KG):
            ks = pl.ds(k * BS, BS)
            gate += jnp.dot(p_ref[0, :, col(gr_ref[f, k])], w_ref[f, ks, :], preferred_element_type=f32)
            up += jnp.dot(p_ref[0, :, col(ur_ref[f, k])], w_ref[slots + f, ks, :], preferred_element_type=f32)
            hg += jnp.dot(p_ref[1, :, col(dc_ref[f, k])], w_ref[2 * slots + f, ks, :], preferred_element_type=f32)
        sg = 1.0 / (1.0 + jnp.exp(-gate))
        silu = gate * sg
        hidden = (silu * up).astype(bf16)
        gg = (hg * up * sg * (1.0 + gate * (1.0 - sg))).astype(bf16)
        ug = (hg * silu).astype(bf16)
        for k in range(KG):
            ks = pl.ds(k * BS, BS)
            gt = w_ref[f, ks, :]
            ut = w_ref[slots + f, ks, :]
            dt = w_ref[2 * slots + f, ks, :]
            cd = col(dc_ref[f, k])
            cg = col(gr_ref[f, k])
            cu = col(ur_ref[f, k])
            out_acc[:, cd] += lax.dot_general(hidden, dt, nt, preferred_element_type=f32)
            in_acc[:, cg] += lax.dot_general(gg, gt, nt, preferred_element_type=f32)
            in_acc[:, cu] += lax.dot_general(ug, ut, nt, preferred_element_type=f32)
            tiles_ref[f, ks, :] = lax.dot_general(
                p_ref[0, :, cg], gg, tn, preferred_element_type=f32
            ).astype(bf16)
            tiles_ref[slots + f, ks, :] = lax.dot_general(
                p_ref[0, :, cu], ug, tn, preferred_element_type=f32
            ).astype(bf16)
            tiles_ref[2 * slots + f, ks, :] = lax.dot_general(
                p_ref[1, :, cd], hidden, tn, preferred_element_type=f32
            ).astype(bf16)
        return carry

    lax.fori_loop(0, slots, body, 0)
    panel_ref[0] = out_acc[...].astype(bf16)
    panel_ref[1] = in_acc[...].astype(bf16)


def core(panels, tiles, gate_rows, up_rows, down_columns):
    slots = gate_rows.shape[0]
    rows, width = panels.shape[1], panels.shape[2]
    smem = pl.BlockSpec(memory_space=pltpu.SMEM)
    vmem = pl.BlockSpec(memory_space=pltpu.VMEM)
    flops = 2 * rows * BS * BS * slots * KG * 9
    nbytes = 2 * (2 * panels.size + 2 * tiles.size)
    return pl.pallas_call(
        functools.partial(core_kernel, slots),
        out_shape=(
            jax.ShapeDtypeStruct((2, rows, width), jnp.bfloat16),
            jax.ShapeDtypeStruct(tiles.shape, jnp.bfloat16),
        ),
        in_specs=[smem, smem, smem, vmem, vmem],
        out_specs=(vmem, vmem),
        scratch_shapes=[
            pltpu.VMEM((rows, width), jnp.float32),
            pltpu.VMEM((rows, width), jnp.float32),
        ],
        compiler_params=pltpu.CompilerParams(vmem_limit_bytes=62 * 1024 * 1024),
        cost_estimate=pl.CostEstimate(
            flops=flops, transcendentals=rows * BS * slots, bytes_accessed=nbytes
        ),
    )(gate_rows, up_rows, down_columns, panels, tiles)


def shards(tokens, out_grad, gate_weight, up_weight, down_weight, gate_rows, up_rows, down_columns):
    owned_slots = gate_weight.shape[0]
    panels = lax.all_gather(jnp.stack([tokens, out_grad]), "col", axis=2, tiled=True)
    tiles = lax.all_gather(
        jnp.concatenate([gate_weight, up_weight, down_weight], axis=0), "row", axis=1, tiled=True
    )
    panel_part, tile_part = core(panels, tiles, gate_rows, up_rows, down_columns)
    tile_sums = lax.psum_scatter(tile_part, "row", scatter_dimension=1, tiled=True)
    panel_sums = lax.psum_scatter(panel_part, "col", scatter_dimension=2, tiled=True)
    return (
        panel_sums[0],
        panel_sums[1],
        tile_sums[:owned_slots],
        tile_sums[owned_slots : 2 * owned_slots],
        tile_sums[2 * owned_slots :],
    )


def solution(mesh):
    in_specs = (
        P("row", "col"),
        P("row", "col"),
        P("col", "row", None),
        P("col", "row", None),
        P("col", "row", None),
        P("col", None),
        P("col", None),
        P("col", None),
    )
    out_specs = (
        P("row", "col"),
        P("row", "col"),
        P("col", "row", None),
        P("col", "row", None),
        P("col", "row", None),
    )
    return jax.shard_map(shards, mesh=mesh, in_specs=in_specs, out_specs=out_specs, check_vma=False)
```

time: 437 us -> 333 us (0.76)
  local copies, waits for them, and re-layouts: 102 us -> 3.59 us
  other arithmetic: 91 us -> 3.67 us
  waiting for transfers between devices: 203 us -> 285 us
  Pallas kernels: 0 us -> 25.1 us
  matrix products: 24.6 us -> 0 us
    reduce_scatter x2, waiting for transfers between devices: 88.1 us -> 155 us  [the longest x1 97 us: shards(): lax.psum_scatter(panel_part, 'col', scatter_dimension=2, tiled=True)]
    scatter-add x3 -> x0, other arithmetic: 56.9 us -> none  [spread(): zero_block.at[:, block_lists.reshape(-1)]]
    another operation x7 -> x0, local copies, waits for them, and re-layouts: 38.3 us -> none
    reshape x9 -> x0, local copies, waits for them, and re-layouts: 26.3 us -> none  [the longest x3 25.1 us: spread(): contrib.reshape(rows_here, -1, BS)]
    pallas_call x0 -> x1, Pallas kernels: none -> 25.1 us  [core(): pl.pallas_call(functools.partial(core_kernel, slots), out_shape=(jax.Shap...]
    dot_general x9 -> x0, matrix products: 24.6 us -> none  [the longest x1 5.61 us: shards(): jnp.einsum('tfi,fkri->tfkr', gate_grad, gate_four, preferred_element_type...]
    another operation x3 -> x0, other arithmetic: 23.1 us -> none
    gather x3 -> x0, local copies, waits for them, and re-layouts: 15.2 us -> none  [the longest x1 5.08 us: shards(): jnp.take(blocks_grad, down_columns.reshape(-1), axis=1)]
  transfers between devices with their start and end apart: 4 -> 4, of which waited for: 3 -> 4; matrix products, arithmetic and copies ran while one was open for 36% -> 1% of each run, Pallas kernels for 0% -> 0%
where the time goes in v2:
time: 333 us; the launch traced here: 332 us
  waiting for transfers between devices  285 us (86%)
  Pallas kernels  25.1 us (8%)
  between operations  13.8 us (4%)
  other arithmetic  3.67 us (1%)
  local copies, waits for them, and re-layouts  3.59 us (1%)
    reduce_scatter x1, waiting for transfers between devices, shards(): lax.psum_scatter(panel_part, 'col', scatter_dimension=2, tiled=True)  97 us
    all_gather x1, waiting for transfers between devices, shards(): lax.all_gather(jnp.stack([tokens, out_grad]), 'col', axis=2, tiled=True)  85.3 us
    reduce_scatter x1, waiting for transfers between devices, shards(): lax.psum_scatter(tile_part, 'row', scatter_dimension=1, tiled=True)  58.4 us
    all_gather x1, waiting for transfers between devices, shards(): lax.all_gather(jnp.concatenate([gate_weight, up_weight, down_weight], axi...  44.2 us
    pallas_call x1, Pallas kernels, core(): pl.pallas_call(functools.partial(core_kernel, slots), out_shape=(jax.Shap...  25.1 us
  transfers between devices with their start and end apart: 4, of which 4 were waited for; matrix products, arithmetic and copies ran while one was open for 1% of the time, Pallas kernels for 0%

profile of v2, /device:TPU:64, one launch (start us, length us, event | category | flops | bytes accessed | tf_op | source)
XLA Modules:
  0.0 331.8 jit_solution(16195672962272929977)
XLA Ops:
  7.2 0.0 all-gather.5.cloned.1.call-start
  7.2 1.8 pad_maximum_fusion.1
  9.0 0.0 all-gather.5.cloned.1.call-update
  9.0 0.0 all-gather.3.cloned.1.call-start
  9.1 1.9 pad_maximum_fusion
  11.0 0.0 all-gather.3.cloned.1.call-update
  11.0 0.0 reduce-scatter.5.cloned.1.call-start
  11.0 44.2 %all-gather.5.cloned.1.call-done.w_ref = bf16[21,1024,128]{2,1,0:T(8,128)(2,1)} async-done(((bf16[21,64,128]{2,1,0:T(8,128)(2,1)}), bf16[21,1024,128]{2,1,0:T(8,128)(2,1)}) %all-gather.5.cloned.1.call-update) | async-done | bytes 5505040 | tf_op jit(solution)/shard_map/all_gather | solution.py:97
  55.2 85.3 %all-gather.3.cloned.1.call-done.p_ref = bf16[2,256,8192]{2,1,0:T(8,128)(2,1)} async-done(((bf16[2,256,512]{2,1,0:T(8,128)(2,1)}), bf16[2,256,8192]{2,1,0:T(8,128)(2,1)}) %all-gather.3.cloned.1.call-update) | async-done | bytes 8388624 | tf_op jit(solution)/shard_map/all_gather | solution.py:96
  140.5 25.1 %shard_map.119 = (bf16[2,256,8192]{2,1,0:T(8,128)(2,1)}, bf16[21,1024,128]{2,1,0:T(8,128)(2,1)}) custom-call(s32[7,8]{1,0:T(8,128)} %gr_ref.1, s32[7,8]{1,0:T(8,128)} %ur_ref.1, s32[7,8]{1,0:T(8,128)} %dc_ref.1, bf16[2,256,8192]{2,1,0:T(8,128)(2,1)} %all-gather.3.cloned.1.call-done.p_ref, bf16[21,1024,128]{2,1,0:T(8,128)(2,1)} %all-gather.5.cloned.1.call-done.w_ref), custom_call_target="tpu_custom_call" | custom-call | flops 4227858432 | bytes 27787264 | tf_op jit(solution)/shard_map/pallas_call | solution.py:75
  165.7 0.0 reduce-scatter.5.cloned.1.call-update
  165.7 0.0 reduce-scatter.3.cloned.1.call-start
  165.8 0.5 reduce-scatter.3.cloned.1.call-update
  166.3 58.4 %reduce-scatter.5.cloned.1.call-done = bf16[21,64,128]{2,1,0:T(8,128)(2,1)} async-done(((bf16[21,1024,128]{2,1,0:T(8,128)(2,1)}), bf16[21,64,128]{2,1,0:T(8,128)(2,1)}) %reduce-scatter.5.cloned.1.call-update) | async-done | bytes 344080 | tf_op jit(solution)/shard_map/reduce_scatter | solution.py:101
  224.7 1.7 fusion
  226.4 97.0 %reduce-scatter.3.cloned.1.call-done = bf16[2,256,512]{2,1,0:T(8,128)(2,1)} async-done(((bf16[2,256,8192]{2,1,0:T(8,128)(2,1)}), bf16[2,256,512]{2,1,0:T(8,128)(2,1)}) %reduce-scatter.3.cloned.1.call-update) | async-done | bytes 524304 | tf_op jit(solution)/shard_map/reduce_scatter | solution.py:102
  323.4 1.9 slice_bitcast_fusion
Async XLA Ops:
  7.2 48.1 %all-gather.5.cloned.1.call-start = ((), (), s32[]{:S(2)}) async-start(), calls=%async_computation.3 | async-start | bytes 5849088 | tf_op jit(solution)/shard_map/all_gather | solution.py:97
  9.0 131.5 %all-gather.3.cloned.1.call-start = ((), (), s32[]{:S(2)}) async-start(), calls=%async_computation.2 | async-start | bytes 8912896 | tf_op jit(solution)/shard_map/all_gather | solution.py:96
  11.0 213.7 %reduce-scatter.5.cloned.1.call-start = ((), (), s32[]{:S(2)}) async-start(), calls=%async_computation.5 | async-start | bytes 5849088 | tf_op jit(solution)/shard_map/reduce_scatter | solution.py:101
  165.7 157.7 %reduce-scatter.3.cloned.1.call-start = ((), (), s32[]{:S(2)}) async-start(), calls=%async_computation.4 | async-start | bytes 8912896 | tf_op jit(solution)/shard_map/reduce_scatter | solution.py:102
Sparse Core Ops, SparseCore 0:
  9.9 45.3 all-gather.4
  57.6 82.8 all-gather.2
  165.8 58.8 reduce-scatter.4
  228.7 94.6 reduce-scatter.2

commit v3 on v2

--- a/solution.py
+++ b/solution.py
@@ -10,6 +10,105 @@
 BS = 128
 KG = 8
 KH = 8
+
+
+MESH = pl.DeviceIdType.MESH
+
+
+def gather_rows_kernel(n_row, w_ref, out_ref, lsem, psend, precv, rsend, rrecv, fsend, frecv):
+    me = lax.axis_index("row")
+    n_chip = n_row // 2
+    z = me // 2
+    c = me % 2
+    step_dir = 1 - 2 * c
+    partner = z * 2 + (1 - c)
+    nxt = ((z + step_dir + n_chip) % n_chip) * 2 + c
+    prv = ((z - step_dir + n_chip) % n_chip) * 2 + c
+    half = w_ref.shape[1]
+    tile = 2 * half
+
+    barrier = pltpu.get_barrier_semaphore()
+    for peer in (partner, nxt, prv):
+        pl.semaphore_signal(barrier, inc=1, device_id={"row": peer}, device_id_type=MESH)
+    pl.semaphore_wait(barrier, 3)
+
+    def chip_tile(p):
+        return out_ref.at[:, pl.ds(pl.multiple_of(p * tile, tile), tile), :]
+
+    own = out_ref.at[:, pl.ds(pl.multiple_of(z * tile + c * half, half), half), :]
+    local = pltpu.make_async_copy(w_ref, own, lsem)
+    local.start()
+    swap = pltpu.make_async_remote_copy(
+        src_ref=w_ref, dst_ref=own, send_sem=psend, recv_sem=precv,
+        device_id={"row": partner}, device_id_type=MESH,
+    )
+    swap.start()
+    local.wait()
+    theirs = out_ref.at[:, pl.ds(pl.multiple_of(z * tile + (1 - c) * half, half), half), :]
+    pltpu.make_async_remote_copy(
+        src_ref=w_ref, dst_ref=theirs, send_sem=psend, recv_sem=precv,
+        device_id={"row": partner}, device_id_type=MESH,
+    ).wait_recv()
+    swap.wait_send()
+
+    steps = n_chip // 2
+    sends = []
+    fwds = []
+    for s in range(1, steps + 1):
+        p_send = (z - (s - 1) * step_dir + n_chip * steps) % n_chip
+        p_recv = (z - s * step_dir + n_chip * steps) % n_chip
+        ring = pltpu.make_async_remote_copy(
+            src_ref=chip_tile(p_send), dst_ref=chip_tile(p_send),
+            send_sem=rsend.at[s - 1], recv_sem=rrecv.at[s - 1],
+            device_id={"row": nxt}, device_id_type=MESH,
+        )
+        ring.start()
+        sends.append(ring)
+        pltpu.make_async_remote_copy(
+            src_ref=chip_tile(p_recv), dst_ref=chip_tile(p_recv),
+            send_sem=rsend.at[s - 1], recv_sem=rrecv.at[s - 1],
+            device_id={"row": prv}, device_id_type=MESH,
+        ).wait_recv()
+        if s < steps:
+            fwd = pltpu.make_async_remote_copy(
+                src_ref=chip_tile(p_recv), dst_ref=chip_tile(p_recv),
+                send_sem=fsend.at[s - 1], recv_sem=frecv.at[s - 1],
+                device_id={"row": partner}, device_id_type=MESH,
+            )
+            fwd.start()
+            fwds.append(fwd)
+    for s in range(1, steps):
+        p_in = (z + s * step_dir + n_chip * steps) % n_chip
+        pltpu.make_async_remote_copy(
+            src_ref=chip_tile(p_in), dst_ref=chip_tile(p_in),
+            send_sem=fsend.at[s - 1], recv_sem=frecv.at[s - 1],
+            device_id={"row": partner}, device_id_type=MESH,
+        ).wait_recv()
+    for cp in sends + fwds:
+        cp.wait_send()
+
+
+def gather_rows(w, n_row):
+    slots, half, width = w.shape
+    steps = n_row // 4
+    any_spec = pl.BlockSpec(memory_space=pl.ANY)
+    return pl.pallas_call(
+        functools.partial(gather_rows_kernel, n_row),
+        out_shape=jax.ShapeDtypeStruct((slots, half * n_row, width), w.dtype),
+        in_specs=[any_spec],
+        out_specs=any_spec,
+        scratch_shapes=[
+            pltpu.SemaphoreType.DMA(()),
+            pltpu.SemaphoreType.DMA(()),
+            pltpu.SemaphoreType.DMA(()),
+            pltpu.SemaphoreType.DMA((steps,)),
+            pltpu.SemaphoreType.DMA((steps,)),
+            pltpu.SemaphoreType.DMA((steps - 1,)),
+            pltpu.SemaphoreType.DMA((steps - 1,)),
+        ],
+        compiler_params=pltpu.CompilerParams(collective_id=0, has_side_effects=True),
+        cost_estimate=pl.CostEstimate(flops=0, transcendentals=0, bytes_accessed=2 * w.size * n_row),
+    )(w)
 
 
 def core_kernel(slots, gr_ref, ur_ref, dc_ref, p_ref, w_ref, panel_ref, tiles_ref, out_acc, in_acc):
@@ -94,9 +193,8 @@
 def shards(tokens, out_grad, gate_weight, up_weight, down_weight, gate_rows, up_rows, down_columns):
     owned_slots = gate_weight.shape[0]
     panels = lax.all_gather(jnp.stack([tokens, out_grad]), "col", axis=2, tiled=True)
-    tiles = lax.all_gather(
-        jnp.concatenate([gate_weight, up_weight, down_weight], axis=0), "row", axis=1, tiled=True
-    )
+    n_row = lax.axis_size("row")
+    tiles = gather_rows(jnp.concatenate([gate_weight, up_weight, down_weight], axis=0), n_row)
     panel_part, tile_part = core(panels, tiles, gate_rows, up_rows, down_columns)
     tile_sums = lax.psum_scatter(tile_part, "row", scatter_dimension=1, tiled=True)
     panel_sums = lax.psum_scatter(panel_part, "col", scatter_dimension=2, tiled=True)

time: 333 us -> 288 us (0.86)
  waiting for transfers between devices: 285 us -> 184 us
  Pallas kernels: 25.1 us -> 81.8 us
    all_gather x1, waiting for transfers between devices: 85.3 us -> 28.3 us  [shards(): lax.all_gather(jnp.stack([tokens, out_grad]), 'col', axis=2, tiled=True)]
    pallas_call x0 -> x1, Pallas kernels: none -> 56.7 us  [gather_rows(): pl.pallas_call(functools.partial(gather_rows_kernel, n_row), out_shape=ja...]
    all_gather x1 -> x0, waiting for transfers between devices: 44.2 us -> none  [shards(): lax.all_gather(jnp.concatenate([gate_weight, up_weight, down_weight], axi...]
  transfers between devices with their start and end apart: 4 -> 3, of which waited for: 4 -> 3; matrix products, arithmetic and copies ran while one was open for 1% -> 1% of each run, Pallas kernels for 0% -> 20%
where the time goes in v3:
time: 288 us; the launch traced here: 287 us
  waiting for transfers between devices  184 us (64%)
  Pallas kernels  81.8 us (28%)
  between operations  13.8 us (5%)
  other arithmetic  3.73 us (1%)
  local copies, waits for them, and re-layouts  3.59 us (1%)
    reduce_scatter x1, waiting for transfers between devices, shards(): lax.psum_scatter(panel_part, 'col', scatter_dimension=2, tiled=True)  97.1 us
    reduce_scatter x1, waiting for transfers between devices, shards(): lax.psum_scatter(tile_part, 'row', scatter_dimension=1, tiled=True)  58.2 us
    pallas_call x1, Pallas kernels, gather_rows(): pl.pallas_call(functools.partial(gather_rows_kernel, n_row), out_shape=ja...  56.7 us
    all_gather x1, waiting for transfers between devices, shards(): lax.all_gather(jnp.stack([tokens, out_grad]), 'col', axis=2, tiled=True)  28.3 us
    pallas_call x1, Pallas kernels, core(): pl.pallas_call(functools.partial(core_kernel, slots), out_shape=(jax.Shap...  25.1 us
  transfers between devices with their start and end apart: 3, of which 3 were waited for; matrix products, arithmetic and copies ran while one was open for 1% of the time, Pallas kernels for 20%

profile of v3, /device:TPU:64, one launch (start us, length us, event | category | flops | bytes accessed | tf_op | source)
XLA Modules:
  0.0 287.3 jit_solution(13675651243214909593)
XLA Ops:
  7.2 0.0 all-gather.2.cloned.1.call-start
  7.2 1.9 pad_maximum_fusion
  9.1 0.0 all-gather.2.cloned.1.call-update
  9.1 0.0 reduce-scatter.5.cloned.1.call-start
  9.2 1.8 pad_maximum_fusion.1.w_ref
  11.0 56.7 %shard_map.119.w_ref = bf16[21,1024,128]{2,1,0:T(8,128)(2,1)} custom-call(bf16[21,64,128]{2,1,0:T(8,128)(2,1)} %pad_maximum_fusion.1.w_ref), custom_call_target="tpu_custom_call" | custom-call | bytes 5505024 | tf_op jit(solution)/shard_map/pallas_call | solution.py:95
  67.7 28.3 %all-gather.2.cloned.1.call-done.p_ref = bf16[2,256,8192]{2,1,0:T(8,128)(2,1)} async-done(((bf16[2,256,512]{2,1,0:T(8,128)(2,1)}), bf16[2,256,8192]{2,1,0:T(8,128)(2,1)}) %all-gather.2.cloned.1.call-update) | async-done | bytes 8388624 | tf_op jit(solution)/shard_map/all_gather | solution.py:195
  96.0 25.1 %shard_map.120 = (bf16[2,256,8192]{2,1,0:T(8,128)(2,1)}, bf16[21,1024,128]{2,1,0:T(8,128)(2,1)}) custom-call(s32[7,8]{1,0:T(8,128)} %gr_ref.1, s32[7,8]{1,0:T(8,128)} %ur_ref.1, s32[7,8]{1,0:T(8,128)} %dc_ref.1, bf16[2,256,8192]{2,1,0:T(8,128)(2,1)} %all-gather.2.cloned.1.call-done.p_ref, bf16[21,1024,128]{2,1,0:T(8,128)(2,1)} %shard_map.119.w_ref), custom_call_target="tpu_custom_call" | custom-call | flops 4227858432 | bytes 27787264 | tf_op jit(solution)/shard_map/pallas_call | solution.py:174
  121.1 0.0 reduce-scatter.5.cloned.1.call-update
  121.1 0.0 reduce-scatter.3.cloned.1.call-start
  121.2 0.7 reduce-scatter.3.cloned.1.call-update
  121.9 58.2 %reduce-scatter.5.cloned.1.call-done = bf16[21,64,128]{2,1,0:T(8,128)(2,1)} async-done(((bf16[21,1024,128]{2,1,0:T(8,128)(2,1)}), bf16[21,64,128]{2,1,0:T(8,128)(2,1)}) %reduce-scatter.5.cloned.1.call-update) | async-done | bytes 344080 | tf_op jit(solution)/shard_map/reduce_scatter | solution.py:199
  180.1 1.7 fusion
  181.8 97.1 %reduce-scatter.3.cloned.1.call-done = bf16[2,256,512]{2,1,0:T(8,128)(2,1)} async-done(((bf16[2,256,8192]{2,1,0:T(8,128)(2,1)}), bf16[2,256,512]{2,1,0:T(8,128)(2,1)}) %reduce-scatter.3.cloned.1.call-update) | async-done | bytes 524304 | tf_op jit(solution)/shard_map/reduce_scatter | solution.py:200
  278.9 1.9 slice_bitcast_fusion
Async XLA Ops:
  7.2 88.9 %all-gather.2.cloned.1.call-start = ((), (), s32[]{:S(2)}) async-start(), calls=%async_computation.2 | async-start | bytes 8912896 | tf_op jit(solution)/shard_map/all_gather | solution.py:195
  9.1 170.9 %reduce-scatter.5.cloned.1.call-start = ((), (), s32[]{:S(2)}) async-start(), calls=%async_computation.4 | async-start | bytes 5849088 | tf_op jit(solution)/shard_map/reduce_scatter | solution.py:199
  121.1 157.8 %reduce-scatter.3.cloned.1.call-start = ((), (), s32[]{:S(2)}) async-start(), calls=%async_computation.3 | async-start | bytes 8912896 | tf_op jit(solution)/shard_map/reduce_scatter | solution.py:200
Sparse Core Ops, SparseCore 0:
  10.4 85.5 all-gather.1
  121.3 58.7 reduce-scatter.4
  184.2 94.6 reduce-scatter.2

commit v4 on v3

--- a/solution.py
+++ b/solution.py
@@ -111,6 +111,82 @@
     )(w)
 
 
+def scatter_rows_kernel(n_row, x_ref, out_ref, part_buf, send_buf, recv_buf, psend, precv, rsend, rrecv):
+    me = lax.axis_index("row")
+    n_chip = n_row // 2
+    z = me // 2
+    c = me % 2
+    step_dir = 1 - 2 * c
+    partner = z * 2 + (1 - c)
+    nxt = ((z + step_dir + n_chip) % n_chip) * 2 + c
+    prv = ((z - step_dir + n_chip) % n_chip) * 2 + c
+    f32 = jnp.float32
+
+    barrier = pltpu.get_barrier_semaphore()
+    for peer in (partner, nxt, prv):
+        pl.semaphore_signal(barrier, inc=1, device_id={"row": peer}, device_id_type=MESH)
+    pl.semaphore_wait(barrier, 3)
+
+    swap = pltpu.make_async_remote_copy(
+        src_ref=x_ref.at[:, :, 1 - c], dst_ref=part_buf, send_sem=psend, recv_sem=precv,
+        device_id={"row": partner}, device_id_type=MESH,
+    )
+    swap.start()
+    swap.wait_recv()
+
+    def chip_part(q):
+        return x_ref[:, q, c].astype(f32) + part_buf[:, q].astype(f32)
+
+    sends = []
+    for s in range(1, n_chip):
+        q = (z - s * step_dir + n_chip * n_chip) % n_chip
+        if s == 1:
+            send_buf[s - 1] = chip_part(q)
+        else:
+            send_buf[s - 1] = recv_buf[s - 2] + chip_part(q)
+        ring = pltpu.make_async_remote_copy(
+            src_ref=send_buf.at[s - 1], dst_ref=recv_buf.at[s - 1],
+            send_sem=rsend.at[s - 1], recv_sem=rrecv.at[s - 1],
+            device_id={"row": nxt}, device_id_type=MESH,
+        )
+        ring.start()
+        sends.append(ring)
+        ring.wait_recv()
+    out_ref[...] = (recv_buf[n_chip - 2] + chip_part(z)).astype(out_ref.dtype)
+    swap.wait_send()
+    for cp in sends:
+        cp.wait_send()
+
+
+def scatter_rows(x, n_row):
+    slots, height, width = x.shape
+    n_chip = n_row // 2
+    half = height // n_row
+    x5 = x.reshape(slots, n_chip, 2, half, width)
+    vmem = pl.BlockSpec(memory_space=pltpu.VMEM)
+    return pl.pallas_call(
+        functools.partial(scatter_rows_kernel, n_row),
+        out_shape=jax.ShapeDtypeStruct((slots, half, width), x.dtype),
+        in_specs=[vmem],
+        out_specs=vmem,
+        scratch_shapes=[
+            pltpu.VMEM((slots, n_chip, half, width), x.dtype),
+            pltpu.VMEM((n_chip - 1, slots, half, width), jnp.float32),
+            pltpu.VMEM((n_chip - 1, slots, half, width), jnp.float32),
+            pltpu.SemaphoreType.DMA(()),
+            pltpu.SemaphoreType.DMA(()),
+            pltpu.SemaphoreType.DMA((n_chip - 1,)),
+            pltpu.SemaphoreType.DMA((n_chip - 1,)),
+        ],
+        compiler_params=pltpu.CompilerParams(
+            collective_id=1, has_side_effects=True, vmem_limit_bytes=48 * 1024 * 1024
+        ),
+        cost_estimate=pl.CostEstimate(
+            flops=x.size, transcendentals=0, bytes_accessed=4 * x.size
+        ),
+    )(x5)
+
+
 def core_kernel(slots, gr_ref, ur_ref, dc_ref, p_ref, w_ref, panel_ref, tiles_ref, out_acc, in_acc):
     out_acc[...] = jnp.zeros_like(out_acc)
     in_acc[...] = jnp.zeros_like(in_acc)
@@ -196,7 +272,7 @@
     n_row = lax.axis_size("row")
     tiles = gather_rows(jnp.concatenate([gate_weight, up_weight, down_weight], axis=0), n_row)
     panel_part, tile_part = core(panels, tiles, gate_rows, up_rows, down_columns)
-    tile_sums = lax.psum_scatter(tile_part, "row", scatter_dimension=1, tiled=True)
+    tile_sums = scatter_rows(tile_part, n_row)
     panel_sums = lax.psum_scatter(panel_part, "col", scatter_dimension=2, tiled=True)
     return (
         panel_sums[0],

time: 288 us -> 220 us (0.76)
  waiting for transfers between devices: 184 us -> 36.6 us
  Pallas kernels: 81.8 us -> 160 us
    reduce_scatter x1, waiting for transfers between devices: 97.1 us -> 8.24 us  [shards(): lax.psum_scatter(panel_part, 'col', scatter_dimension=2, tiled=True)]
    pallas_call x0 -> x1, Pallas kernels: none -> 78.1 us  [scatter_rows(): pl.pallas_call(functools.partial(scatter_rows_kernel, n_row), out_shape=j...]
    reduce_scatter x1 -> x0, waiting for transfers between devices: 58.2 us -> none  [shards(): lax.psum_scatter(tile_part, 'row', scatter_dimension=1, tiled=True)]
  transfers between devices with their start and end apart: 3 -> 2, of which waited for: 3 -> 2; matrix products, arithmetic and copies ran while one was open for 1% -> 1% of each run, Pallas kernels for 20% -> 61%
where the time goes in v4:
time: 220 us
  Pallas kernels  160 us (73%)
  waiting for transfers between devices  36.6 us (17%)
  between operations  14.1 us (6%)
  local copies, waits for them, and re-layouts  5.14 us (2%)
  other arithmetic  3.72 us (2%)
    pallas_call x1, Pallas kernels, scatter_rows(): pl.pallas_call(functools.partial(scatter_rows_kernel, n_row), out_shape=j...  78.1 us
    pallas_call x1, Pallas kernels, gather_rows(): pl.pallas_call(functools.partial(gather_rows_kernel, n_row), out_shape=ja...  56.7 us
    all_gather x1, waiting for transfers between devices, shards(): lax.all_gather(jnp.stack([tokens, out_grad]), 'col', axis=2, tiled=True)  28.3 us
    pallas_call x1, Pallas kernels, core(): pl.pallas_call(functools.partial(core_kernel, slots), out_shape=(jax.Shap...  25.1 us
    reduce_scatter x1, waiting for transfers between devices, shards(): lax.psum_scatter(panel_part, 'col', scatter_dimension=2, tiled=True)  8.24 us
  transfers between devices with their start and end apart: 2, of which 2 were waited for; matrix products, arithmetic and copies ran while one was open for 1% of the time, Pallas kernels for 61%

profile of v4, /device:TPU:64, one launch (start us, length us, event | category | flops | bytes accessed | tf_op | source)
XLA Modules:
  0.0 219.5 jit_solution(10029514990855782157)
XLA Ops:
  7.2 0.0 all-gather.2.cloned.1.call-start
  7.2 1.9 pad_maximum_fusion
  9.1 0.0 all-gather.2.cloned.1.call-update
  9.2 0.0 reduce-scatter.2.cloned.1.call-start
  9.2 1.8 pad_maximum_fusion.1.w_ref
  11.0 56.7 %shard_map.119.w_ref = bf16[21,1024,128]{2,1,0:T(8,128)(2,1)} custom-call(bf16[21,64,128]{2,1,0:T(8,128)(2,1)} %pad_maximum_fusion.1.w_ref), custom_call_target="tpu_custom_call" | custom-call | bytes 5505024 | tf_op jit(solution)/shard_map/pallas_call | solution.py:95
  67.7 28.3 %all-gather.2.cloned.1.call-done.p_ref = bf16[2,256,8192]{2,1,0:T(8,128)(2,1)} async-done(((bf16[2,256,512]{2,1,0:T(8,128)(2,1)}), bf16[2,256,8192]{2,1,0:T(8,128)(2,1)}) %all-gather.2.cloned.1.call-update) | async-done | bytes 8388624 | tf_op jit(solution)/shard_map/all_gather | solution.py:271
  96.0 25.1 %shard_map.120 = (bf16[2,256,8192]{2,1,0:T(8,128)(2,1)}, bf16[21,1024,128]{2,1,0:T(8,128)(2,1)}) custom-call(s32[7,8]{1,0:T(8,128)} %gr_ref.1, s32[7,8]{1,0:T(8,128)} %ur_ref.1, s32[7,8]{1,0:T(8,128)} %dc_ref.1, bf16[2,256,8192]{2,1,0:T(8,128)(2,1)} %all-gather.2.cloned.1.call-done.p_ref, bf16[21,1024,128]{2,1,0:T(8,128)(2,1)} %shard_map.119.w_ref), custom_call_target="tpu_custom_call" | custom-call | flops 4227858432 | bytes 27787264 | tf_op jit(solution)/shard_map/pallas_call | solution.py:250
  121.1 0.0 reduce-scatter.2.cloned.1.call-update
  121.1 0.0 copy-start
  121.1 2.6 %copy-done = bf16[21,1024,128]{2,1,0:T(8,128)(2,1)S(1)} copy-done((bf16[21,1024,128]{2,1,0:T(8,128)(2,1)S(1)}, bf16[21,1024,128]{2,1,0:T(8,128)(2,1)}, u32[]{:S(2)}) %copy-start) | copy-done | bytes 5505048
  123.7 78.1 %shard_map.121 = bf16[21,64,128]{2,1,0:T(8,128)(2,1)S(1)} custom-call(bf16[21,8,2,64,128]{4,3,2,1,0:T(8,128)(2,1)S(1)} %bitcast.7), custom_call_target="tpu_custom_call" | custom-call | flops 2752512 | bytes 11010048 | tf_op jit(solution)/shard_map/pallas_call | solution.py:167
  201.8 0.7 fusion
  202.6 8.2 %reduce-scatter.2.cloned.1.call-done = bf16[2,256,512]{2,1,0:T(8,128)(2,1)} async-done(((bf16[2,256,8192]{2,1,0:T(8,128)(2,1)}), bf16[2,256,512]{2,1,0:T(8,128)(2,1)}) %reduce-scatter.2.cloned.1.call-update) | async-done | bytes 524304 | tf_op jit(solution)/shard_map/reduce_scatter | solution.py:276
  210.8 1.9 slice_bitcast_fusion
Async XLA Ops:
  7.2 88.9 %all-gather.2.cloned.1.call-start = ((), (), s32[]{:S(2)}) async-start(), calls=%async_computation.1 | async-start | bytes 8912896 | tf_op jit(solution)/shard_map/all_gather | solution.py:271
  9.2 201.7 %reduce-scatter.2.cloned.1.call-start = ((), (), s32[]{:S(2)}) async-start(), calls=%async_computation.2 | async-start | bytes 8912896 | tf_op jit(solution)/shard_map/reduce_scatter | solution.py:276
  121.1 2.6 %copy-start = (bf16[21,1024,128]{2,1,0:T(8,128)(2,1)S(1)}, bf16[21,1024,128]{2,1,0:T(8,128)(2,1)}, u32[]{:S(2)}) copy-start(bf16[21,1024,128]{2,1,0:T(8,128)(2,1)} %get-tuple-element.8) | copy-start | bytes 16515076
Sparse Core Ops, SparseCore 0:
  10.4 85.5 all-gather.1
  121.3 89.5 reduce-scatter.1

commit v5 on v4

--- a/solution.py
+++ b/solution.py
@@ -192,12 +192,16 @@
     in_acc[...] = jnp.zeros_like(in_acc)
     f32 = jnp.float32
     bf16 = jnp.bfloat16
-    rows = p_ref.shape[1]
+    peers, _, rows, chunk = p_ref.shape
+    per = chunk // BS
     tn = (((0,), (0,)), ((), ()))
     nt = (((1,), (1,)), ((), ()))
 
     def col(b):
         return pl.ds(pl.multiple_of(b * BS, BS), BS)
+
+    def block(which, b):
+        return p_ref[b // per, which, :, pl.ds(pl.multiple_of((b % per) * BS, BS), BS)]
 
     def body(f, carry):
         gate = jnp.zeros((rows, BS), f32)
@@ -205,9 +209,9 @@
         hg = jnp.zeros((rows, BS), f32)
         for k in range(KG):
             ks = pl.ds(k * BS, BS)
-            gate += jnp.dot(p_ref[0, :, col(gr_ref[f, k])], w_ref[f, ks, :], preferred_element_type=f32)
-            up += jnp.dot(p_ref[0, :, col(ur_ref[f, k])], w_ref[slots + f, ks, :], preferred_element_type=f32)
-            hg += jnp.dot(p_ref[1, :, col(dc_ref[f, k])], w_ref[2 * slots + f, ks, :], preferred_element_type=f32)
+            gate += jnp.dot(block(0, gr_ref[f, k]), w_ref[f, ks, :], preferred_element_type=f32)
+            up += jnp.dot(block(0, ur_ref[f, k]), w_ref[slots + f, ks, :], preferred_element_type=f32)
+            hg += jnp.dot(block(1, dc_ref[f, k]), w_ref[2 * slots + f, ks, :], preferred_element_type=f32)
         sg = 1.0 / (1.0 + jnp.exp(-gate))
         silu = gate * sg
         hidden = (silu * up).astype(bf16)
@@ -218,31 +222,34 @@
             gt = w_ref[f, ks, :]
             ut = w_ref[slots + f, ks, :]
             dt = w_ref[2 * slots + f, ks, :]
-            cd = col(dc_ref[f, k])
-            cg = col(gr_ref[f, k])
-            cu = col(ur_ref[f, k])
-            out_acc[:, cd] += lax.dot_general(hidden, dt, nt, preferred_element_type=f32)
-            in_acc[:, cg] += lax.dot_general(gg, gt, nt, preferred_element_type=f32)
-            in_acc[:, cu] += lax.dot_general(ug, ut, nt, preferred_element_type=f32)
+            bd = dc_ref[f, k]
+            bg = gr_ref[f, k]
+            bu = ur_ref[f, k]
+            out_acc[:, col(bd)] += lax.dot_general(hidden, dt, nt, preferred_element_type=f32)
+            in_acc[:, col(bg)] += lax.dot_general(gg, gt, nt, preferred_element_type=f32)
+            in_acc[:, col(bu)] += lax.dot_general(ug, ut, nt, preferred_element_type=f32)
             tiles_ref[f, ks, :] = lax.dot_general(
-                p_ref[0, :, cg], gg, tn, preferred_element_type=f32
+                block(0, bg), gg, tn, preferred_element_type=f32
             ).astype(bf16)
             tiles_ref[slots + f, ks, :] = lax.dot_general(
-                p_ref[0, :, cu], ug, tn, preferred_element_type=f32
+                block(0, bu), ug, tn, preferred_element_type=f32
             ).astype(bf16)
             tiles_ref[2 * slots + f, ks, :] = lax.dot_general(
-                p_ref[1, :, cd], hidden, tn, preferred_element_type=f32
+                block(1, bd), hidden, tn, preferred_element_type=f32
             ).astype(bf16)
         return carry
 
     lax.fori_loop(0, slots, body, 0)
-    panel_ref[0] = out_acc[...].astype(bf16)
-    panel_ref[1] = in_acc[...].astype(bf16)
+    for j in range(peers):
+        cs = pl.ds(j * chunk, chunk)
+        panel_ref[j, 0] = out_acc[:, cs].astype(bf16)
+        panel_ref[j, 1] = in_acc[:, cs].astype(bf16)
 
 
 def core(panels, tiles, gate_rows, up_rows, down_columns):
     slots = gate_rows.shape[0]
-    rows, width = panels.shape[1], panels.shape[2]
+    peers, _, rows, chunk = panels.shape
+    width = peers * chunk
     smem = pl.BlockSpec(memory_space=pltpu.SMEM)
     vmem = pl.BlockSpec(memory_space=pltpu.VMEM)
     flops = 2 * rows * BS * BS * slots * KG * 9
@@ -250,7 +257,7 @@
     return pl.pallas_call(
         functools.partial(core_kernel, slots),
         out_shape=(
-            jax.ShapeDtypeStruct((2, rows, width), jnp.bfloat16),
+            jax.ShapeDtypeStruct(panels.shape, jnp.bfloat16),
             jax.ShapeDtypeStruct(tiles.shape, jnp.bfloat16),
         ),
         in_specs=[smem, smem, smem, vmem, vmem],
@@ -268,12 +275,15 @@
 
 def shards(tokens, out_grad, gate_weight, up_weight, down_weight, gate_rows, up_rows, down_columns):
     owned_slots = gate_weight.shape[0]
-    panels = lax.all_gather(jnp.stack([tokens, out_grad]), "col", axis=2, tiled=True)
+    panels = lax.all_gather(jnp.stack([tokens, out_grad]), "col", axis=0)
     n_row = lax.axis_size("row")
     tiles = gather_rows(jnp.concatenate([gate_weight, up_weight, down_weight], axis=0), n_row)
     panel_part, tile_part = core(panels, tiles, gate_rows, up_rows, down_columns)
     tile_sums = scatter_rows(tile_part, n_row)
-    panel_sums = lax.psum_scatter(panel_part, "col", scatter_dimension=2, tiled=True)
+    peers, _, rows, chunk = panel_part.shape
+    panel_sums = lax.psum_scatter(
+        panel_part.reshape(peers * 2 * rows, chunk), "col", scatter_dimension=0, tiled=True
+    ).reshape(2, rows, chunk)
     return (
         panel_sums[0],
         panel_sums[1],

time: 220 us -> 213 us (0.968)
  waiting for transfers between devices: 36.6 us -> 28.3 us
    all_gather x1, waiting for transfers between devices: 28.3 us -> 20.8 us  [shards(): panels = lax.all_gather(jnp.stack([tokens, out_grad]), 'col', axis=0)]
  transfers between devices with their start and end apart: 2 -> 2, of which waited for: 2 -> 2; matrix products, arithmetic and copies ran while one was open for 1% -> 1% of each run, Pallas kernels for 61% -> 64%
where the time goes in v5:
time: 213 us; the launch traced here: 212 us
  Pallas kernels  161 us (76%)
  waiting for transfers between devices  28.3 us (13%)
  between operations  14.1 us (7%)
  local copies, waits for them, and re-layouts  5.14 us (2%)
  other arithmetic  3.72 us (2%)
    pallas_call x1, Pallas kernels, scatter_rows(): pl.pallas_call(functools.partial(scatter_rows_kernel, n_row), out_shape=j...  79 us
    pallas_call x1, Pallas kernels, gather_rows(): pl.pallas_call(functools.partial(gather_rows_kernel, n_row), out_shape=ja...  56.7 us
    pallas_call x1, Pallas kernels, core(): pl.pallas_call(functools.partial(core_kernel, slots), out_shape=(jax.Shap...  24.9 us
    all_gather x1, waiting for transfers between devices, shards(): panels = lax.all_gather(jnp.stack([tokens, out_grad]), 'col', axis=0)  20.8 us
    reduce_scatter x1, waiting for transfers between devices, shards(): lax.psum_scatter(panel_part.reshape(peers * 2 * rows, chunk), 'col', scat...  7.52 us
  transfers between devices with their start and end apart: 2, of which 2 were waited for; matrix products, arithmetic and copies ran while one was open for 1% of the time, Pallas kernels for 64%

profile of v5, /device:TPU:64, one launch (start us, length us, event | category | flops | bytes accessed | tf_op | source)
XLA Modules:
  0.0 211.9 jit_solution(8716399294258911901)
XLA Ops:
  7.2 0.0 all-gather.3.cloned.1.call-start
  7.2 1.9 pad_maximum_fusion
  9.1 0.0 all-gather.3.cloned.1.call-update
  9.2 0.0 reduce-scatter.2.cloned.1.call-start
  9.2 1.8 pad_maximum_fusion.1.w_ref
  11.0 56.7 %shard_map.119.w_ref = bf16[21,1024,128]{2,1,0:T(8,128)(2,1)} custom-call(bf16[21,64,128]{2,1,0:T(8,128)(2,1)} %pad_maximum_fusion.1.w_ref), custom_call_target="tpu_custom_call" | custom-call | bytes 5505024 | tf_op jit(solution)/shard_map/pallas_call | solution.py:95
  67.7 20.8 %all-gather.3.cloned.1.call-done = bf16[32,256,512]{2,1,0:T(8,128)(2,1)} async-done(((bf16[2,256,512]{2,1,0:T(8,128)(2,1)}), bf16[32,256,512]{2,1,0:T(8,128)(2,1)}) %all-gather.3.cloned.1.call-update) | async-done | bytes 8388624 | tf_op jit(solution)/shard_map/all_gather | solution.py:278
  88.5 24.9 %shard_map.120 = (bf16[16,2,256,512]{3,2,1,0:T(8,128)(2,1)}, bf16[21,1024,128]{2,1,0:T(8,128)(2,1)}) custom-call(s32[7,8]{1,0:T(8,128)} %gr_ref.1, s32[7,8]{1,0:T(8,128)} %ur_ref.1, s32[7,8]{1,0:T(8,128)} %dc_ref.1, bf16[16,2,256,512]{3,2,1,0:T(8,128)(2,1)} %bitcast.9, bf16[21,1024,128]{2,1,0:T(8,128)(2,1)} %shard_map.119.w_ref), custom_call_target="tpu_custom_call" | custom-call | flops 4227858432 | bytes 27787264 | tf_op jit(solution)/shard_map/pallas_call | solution.py:257
  113.3 0.0 reduce-scatter.2.cloned.1.call-update
  113.4 0.0 copy-start
  113.4 2.6 %copy-done = bf16[21,1024,128]{2,1,0:T(8,128)(2,1)S(1)} copy-done((bf16[21,1024,128]{2,1,0:T(8,128)(2,1)S(1)}, bf16[21,1024,128]{2,1,0:T(8,128)(2,1)}, u32[]{:S(2)}) %copy-start) | copy-done | bytes 5505048
  115.9 79.0 %shard_map.121 = bf16[21,64,128]{2,1,0:T(8,128)(2,1)S(1)} custom-call(bf16[21,8,2,64,128]{4,3,2,1,0:T(8,128)(2,1)S(1)} %bitcast.5), custom_call_target="tpu_custom_call" | custom-call | flops 2752512 | bytes 11010048 | tf_op jit(solution)/shard_map/pallas_call | solution.py:167
  194.9 0.7 fusion.1
  195.7 7.5 %reduce-scatter.2.cloned.1.call-done = bf16[512,512]{1,0:T(8,128)(2,1)} async-done(((bf16[8192,512]{1,0:T(8,128)(2,1)}), bf16[512,512]{1,0:T(8,128)(2,1)}) %reduce-scatter.2.cloned.1.call-update) | async-done | bytes 524304 | tf_op jit(solution)/shard_map/reduce_scatter | solution.py:284
  203.2 1.9 fusion
Async XLA Ops:
  7.2 81.3 %all-gather.3.cloned.1.call-start = ((), (), s32[]{:S(2)}) async-start(), calls=%async_computation.2 | async-start | bytes 8912896 | tf_op jit(solution)/shard_map/all_gather | solution.py:278
  9.2 194.0 %reduce-scatter.2.cloned.1.call-start = ((), (), s32[]{:S(2)}) async-start(), calls=%async_computation.1 | async-start | bytes 8912896 | tf_op jit(solution)/shard_map/reduce_scatter | solution.py:284
  113.4 2.6 %copy-start = (bf16[21,1024,128]{2,1,0:T(8,128)(2,1)S(1)}, bf16[21,1024,128]{2,1,0:T(8,128)(2,1)}, u32[]{:S(2)}) copy-start(bf16[21,1024,128]{2,1,0:T(8,128)(2,1)} %get-tuple-element.8) | copy-start | bytes 16515076
Sparse Core Ops, SparseCore 0:
  10.4 77.9 all-gather.2
  113.5 89.6 reduce-scatter.1

commit v6 on v5

--- a/solution.py
+++ b/solution.py
@@ -280,10 +280,8 @@
     tiles = gather_rows(jnp.concatenate([gate_weight, up_weight, down_weight], axis=0), n_row)
     panel_part, tile_part = core(panels, tiles, gate_rows, up_rows, down_columns)
     tile_sums = scatter_rows(tile_part, n_row)
-    peers, _, rows, chunk = panel_part.shape
-    panel_sums = lax.psum_scatter(
-        panel_part.reshape(peers * 2 * rows, chunk), "col", scatter_dimension=0, tiled=True
-    ).reshape(2, rows, chunk)
+    received = lax.all_to_all(panel_part, "col", 0, 0, tiled=True)
+    panel_sums = jnp.sum(received.astype(jnp.float32), axis=0).astype(jnp.bfloat16)
     return (
         panel_sums[0],
         panel_sums[1],

time: 213 us -> 281 us (1.32)
  waiting for transfers between devices: 28.3 us -> 86.2 us
  starting transfers between devices: 0.08 us -> 5.32 us
  other arithmetic: 3.72 us -> 8.46 us
    all_to_all x0 -> x1, waiting for transfers between devices: none -> 65.4 us  [shards(): received = lax.all_to_all(panel_part, 'col', 0, 0, tiled=True)]
    reduce_scatter x1 -> x0, waiting for transfers between devices: 7.52 us -> none  [shards(): lax.psum_scatter(panel_part.reshape(peers * 2 * rows, chunk), 'col', scat...]
    all_to_all x0 -> x1, starting transfers between devices: none -> 5.29 us  [shards(): received = lax.all_to_all(panel_part, 'col', 0, 0, tiled=True)]
    reduce_sum x0 -> x1, other arithmetic: none -> 4.74 us  [shards(): jnp.sum(received.astype(jnp.float32), axis=0).astype(jnp.bfloat16)]
  transfers between devices with their start and end apart: 2 -> 2, of which waited for: 2 -> 2; matrix products, arithmetic and copies ran while one was open for 1% -> 1% of each run, Pallas kernels for 64% -> 49%
where the time goes in v6:
time: 281 us; the launch traced here: 278 us
  Pallas kernels  160 us (57%)
  waiting for transfers between devices  86.2 us (31%)
  between operations  14.1 us (5%)
  other arithmetic  8.46 us (3%)
  starting transfers between devices  5.32 us (2%)
  local copies, waits for them, and re-layouts  4.11 us (1%)
    pallas_call x1, Pallas kernels, scatter_rows(): pl.pallas_call(functools.partial(scatter_rows_kernel, n_row), out_shape=j...  78.7 us
    all_to_all x1, waiting for transfers between devices, shards(): received = lax.all_to_all(panel_part, 'col', 0, 0, tiled=True)  65.4 us
    pallas_call x1, Pallas kernels, gather_rows(): pl.pallas_call(functools.partial(gather_rows_kernel, n_row), out_shape=ja...  56.7 us
    pallas_call x1, Pallas kernels, core(): pl.pallas_call(functools.partial(core_kernel, slots), out_shape=(jax.Shap...  24.8 us
    all_gather x1, waiting for transfers between devices, shards(): panels = lax.all_gather(jnp.stack([tokens, out_grad]), 'col', axis=0)  20.8 us
  transfers between devices with their start and end apart: 2, of which 2 were waited for; matrix products, arithmetic and copies ran while one was open for 1% of the time, Pallas kernels for 49%

profile of v6, /device:TPU:64, one launch (start us, length us, event | category | flops | bytes accessed | tf_op | source)
XLA Modules:
  0.0 278.4 jit_solution(6741069390775920622)
XLA Ops:
  7.2 0.0 all-gather.3.cloned.1.call-start
  7.2 1.9 pad_maximum_fusion
  9.1 0.0 all-gather.3.cloned.1.call-update
  9.1 1.8 pad_maximum_fusion.1.w_ref
  11.0 56.7 %shard_map.119.w_ref = bf16[21,1024,128]{2,1,0:T(8,128)(2,1)} custom-call(bf16[21,64,128]{2,1,0:T(8,128)(2,1)} %pad_maximum_fusion.1.w_ref), custom_call_target="tpu_custom_call" | custom-call | bytes 5505024 | tf_op jit(solution)/shard_map/pallas_call | solution.py:95
  67.7 20.8 %all-gather.3.cloned.1.call-done = bf16[32,256,512]{2,1,0:T(8,128)(2,1)} async-done(((bf16[2,256,512]{2,1,0:T(8,128)(2,1)}), bf16[32,256,512]{2,1,0:T(8,128)(2,1)}) %all-gather.3.cloned.1.call-update) | async-done | bytes 8388624 | tf_op jit(solution)/shard_map/all_gather | solution.py:278
  88.5 24.8 %shard_map.120 = (bf16[16,2,256,512]{3,2,1,0:T(8,128)(2,1)}, bf16[21,1024,128]{2,1,0:T(8,128)(2,1)}) custom-call(s32[7,8]{1,0:T(8,128)} %gr_ref.1, s32[7,8]{1,0:T(8,128)} %ur_ref.1, s32[7,8]{1,0:T(8,128)} %dc_ref.1, bf16[16,2,256,512]{3,2,1,0:T(8,128)(2,1)} %bitcast.11, bf16[21,1024,128]{2,1,0:T(8,128)(2,1)} %shard_map.119.w_ref), custom_call_target="tpu_custom_call" | custom-call | flops 4227858432 | bytes 27787264 | tf_op jit(solution)/shard_map/pallas_call | solution.py:257
  113.3 5.3 %all-to-all-start = ((bf16[16,2,256,512]{3,2,1,0:T(8,128)(2,1)}), bf16[16,2,256,512]{3,2,1,0:T(8,128)(2,1)}, u32[]{:S(2)}, u32[]{:S(2)}) async-start(bf16[16,2,256,512]{3,2,1,0:T(8,128)(2,1)} %get-tuple-element.7), calls=%async_computation | async-start | bytes 16777216 | tf_op jit(solution)/shard_map/all_to_all | solution.py:283
  118.6 0.0 copy-start
  118.6 2.6 copy-done
  121.1 78.7 %shard_map.121 = bf16[21,64,128]{2,1,0:T(8,128)(2,1)S(1)} custom-call(bf16[21,8,2,64,128]{4,3,2,1,0:T(8,128)(2,1)S(1)} %bitcast.8), custom_call_target="tpu_custom_call" | custom-call | flops 2752512 | bytes 11010048 | tf_op jit(solution)/shard_map/pallas_call | solution.py:167
  199.9 0.7 fusion
  200.6 65.4 %all-to-all-done = bf16[16,2,256,512]{3,2,1,0:T(8,128)(2,1)} async-done(((bf16[16,2,256,512]{3,2,1,0:T(8,128)(2,1)}), bf16[16,2,256,512]{3,2,1,0:T(8,128)(2,1)}, u32[]{:S(2)}, u32[]{:S(2)}) %all-to-all-start) | async-done | bytes 8388640 | tf_op jit(solution)/shard_map/all_to_all | solution.py:283
  266.0 4.7 %reduce_sum.12 = bf16[2,256,512]{2,1,0:T(8,128)(2,1)S(1)} reduce(bf16[16,2,256,512]{3,2,1,0:T(8,128)(2,1)} %all-to-all-done, bf16[]{:T(256)} %constant.2.clone.1), dimensions={0}, to_apply=%region_0.0 | reduce | flops 3932160 | bytes 8912898 | tf_op jit(solution)/shard_map/reduce_sum | solution.py:284
  270.8 0.8 slice_bitcast_fusion
Async XLA Ops:
  7.2 81.3 %all-gather.3.cloned.1.call-start = ((), (), s32[]{:S(2)}) async-start(), calls=%async_computation.1 | async-start | bytes 8912896 | tf_op jit(solution)/shard_map/all_gather | solution.py:278
  113.3 152.7 %all-to-all-start = ((bf16[16,2,256,512]{3,2,1,0:T(8,128)(2,1)}), bf16[16,2,256,512]{3,2,1,0:T(8,128)(2,1)}, u32[]{:S(2)}, u32[]{:S(2)}) async-start(bf16[16,2,256,512]{3,2,1,0:T(8,128)(2,1)} %get-tuple-element.7), calls=%async_computation | async-start | bytes 16777216 | tf_op jit(solution)/shard_map/all_to_all | solution.py:283
  118.6 2.6 copy-start
Sparse Core Ops, SparseCore 0:
  10.4 77.9 all-gather.2

commit v7 on v5

--- a/solution.py
+++ b/solution.py
@@ -187,63 +187,77 @@
     )(x5)
 
 
-def core_kernel(slots, gr_ref, ur_ref, dc_ref, p_ref, w_ref, panel_ref, tiles_ref, out_acc, in_acc):
-    out_acc[...] = jnp.zeros_like(out_acc)
-    in_acc[...] = jnp.zeros_like(in_acc)
+def core_kernel(
+    slots, gr_ref, ur_ref, dc_ref, p_hbm, w_hbm, panel_hbm, tiles_hbm,
+    p_buf, w_buf, out_acc, in_acc, gath, tstage, pstage, isem, tsem, psem,
+):
     f32 = jnp.float32
     bf16 = jnp.bfloat16
-    peers, _, rows, chunk = p_ref.shape
+    peers, _, rows, chunk = p_buf.shape
     per = chunk // BS
     tn = (((0,), (0,)), ((), ()))
     nt = (((1,), (1,)), ((), ()))
+    cp_w = pltpu.make_async_copy(w_hbm, w_buf, isem.at[0])
+    cp_w.start()
+    cp_p = pltpu.make_async_copy(p_hbm, p_buf, isem.at[1])
+    cp_p.start()
+    out_acc[...] = jnp.zeros_like(out_acc)
+    in_acc[...] = jnp.zeros_like(in_acc)
+    cp_w.wait()
+    cp_p.wait()
 
     def col(b):
         return pl.ds(pl.multiple_of(b * BS, BS), BS)
 
     def block(which, b):
-        return p_ref[b // per, which, :, pl.ds(pl.multiple_of((b % per) * BS, BS), BS)]
+        return p_buf[b // per, which, :, pl.ds(pl.multiple_of((b % per) * BS, BS), BS)]
 
     def body(f, carry):
-        gate = jnp.zeros((rows, BS), f32)
-        up = jnp.zeros((rows, BS), f32)
-        hg = jnp.zeros((rows, BS), f32)
         for k in range(KG):
             ks = pl.ds(k * BS, BS)
-            gate += jnp.dot(block(0, gr_ref[f, k]), w_ref[f, ks, :], preferred_element_type=f32)
-            up += jnp.dot(block(0, ur_ref[f, k]), w_ref[slots + f, ks, :], preferred_element_type=f32)
-            hg += jnp.dot(block(1, dc_ref[f, k]), w_ref[2 * slots + f, ks, :], preferred_element_type=f32)
+            gath[0, :, ks] = block(0, gr_ref[f, k])
+            gath[1, :, ks] = block(0, ur_ref[f, k])
+            gath[2, :, ks] = block(1, dc_ref[f, k])
+        gw = w_buf[f]
+        uw = w_buf[slots + f]
+        dw = w_buf[2 * slots + f]
+        gate = jnp.dot(gath[0], gw, preferred_element_type=f32)
+        up = jnp.dot(gath[1], uw, preferred_element_type=f32)
+        hg = jnp.dot(gath[2], dw, preferred_element_type=f32)
         sg = 1.0 / (1.0 + jnp.exp(-gate))
         silu = gate * sg
         hidden = (silu * up).astype(bf16)
         gg = (hg * up * sg * (1.0 + gate * (1.0 - sg))).astype(bf16)
         ug = (hg * silu).astype(bf16)
+        po = lax.dot_general(hidden, dw, nt, preferred_element_type=f32)
+        pg = lax.dot_general(gg, gw, nt, preferred_element_type=f32)
+        pu = lax.dot_general(ug, uw, nt, preferred_element_type=f32)
         for k in range(KG):
-            ks = pl.ds(k * BS, BS)
-            gt = w_ref[f, ks, :]
-            ut = w_ref[slots + f, ks, :]
-            dt = w_ref[2 * slots + f, ks, :]
-            bd = dc_ref[f, k]
-            bg = gr_ref[f, k]
-            bu = ur_ref[f, k]
-            out_acc[:, col(bd)] += lax.dot_general(hidden, dt, nt, preferred_element_type=f32)
-            in_acc[:, col(bg)] += lax.dot_general(gg, gt, nt, preferred_element_type=f32)
-            in_acc[:, col(bu)] += lax.dot_general(ug, ut, nt, preferred_element_type=f32)
-            tiles_ref[f, ks, :] = lax.dot_general(
-                block(0, bg), gg, tn, preferred_element_type=f32
-            ).astype(bf16)
-            tiles_ref[slots + f, ks, :] = lax.dot_general(
-                block(0, bu), ug, tn, preferred_element_type=f32
-            ).astype(bf16)
-            tiles_ref[2 * slots + f, ks, :] = lax.dot_general(
-                block(1, bd), hidden, tn, preferred_element_type=f32
-            ).astype(bf16)
+            ks = slice(k * BS, (k + 1) * BS)
+            out_acc[:, col(dc_ref[f, k])] += po[:, ks]
+            in_acc[:, col(gr_ref[f, k])] += pg[:, ks]
+            in_acc[:, col(ur_ref[f, k])] += pu[:, ks]
+        tstage[f] = lax.dot_general(gath[0], gg, tn, preferred_element_type=f32).astype(bf16)
+        tstage[slots + f] = lax.dot_general(gath[1], ug, tn, preferred_element_type=f32).astype(bf16)
+        tstage[2 * slots + f] = lax.dot_general(gath[2], hidden, tn, preferred_element_type=f32).astype(bf16)
+        for part in range(3):
+            s = part * slots + f
+            pltpu.make_async_copy(tstage.at[s], tiles_hbm.at[s], tsem.at[s]).start()
         return carry
 
     lax.fori_loop(0, slots, body, 0)
+    outs = []
     for j in range(peers):
         cs = pl.ds(j * chunk, chunk)
-        panel_ref[j, 0] = out_acc[:, cs].astype(bf16)
-        panel_ref[j, 1] = in_acc[:, cs].astype(bf16)
+        pstage[j, 0] = out_acc[:, cs].astype(bf16)
+        pstage[j, 1] = in_acc[:, cs].astype(bf16)
+        cp = pltpu.make_async_copy(pstage.at[j], panel_hbm.at[j], psem.at[j])
+        cp.start()
+        outs.append(cp)
+    for s in range(3 * slots):
+        pltpu.make_async_copy(tstage.at[s], tiles_hbm.at[s], tsem.at[s]).wait()
+    for cp in outs:
+        cp.wait()
 
 
 def core(panels, tiles, gate_rows, up_rows, down_columns):
@@ -251,7 +265,7 @@
     peers, _, rows, chunk = panels.shape
     width = peers * chunk
     smem = pl.BlockSpec(memory_space=pltpu.SMEM)
-    vmem = pl.BlockSpec(memory_space=pltpu.VMEM)
+    any_spec = pl.BlockSpec(memory_space=pl.ANY)
     flops = 2 * rows * BS * BS * slots * KG * 9
     nbytes = 2 * (2 * panels.size + 2 * tiles.size)
     return pl.pallas_call(
@@ -260,11 +274,19 @@
             jax.ShapeDtypeStruct(panels.shape, jnp.bfloat16),
             jax.ShapeDtypeStruct(tiles.shape, jnp.bfloat16),
         ),
-        in_specs=[smem, smem, smem, vmem, vmem],
-        out_specs=(vmem, vmem),
+        in_specs=[smem, smem, smem, any_spec, any_spec],
+        out_specs=(any_spec, any_spec),
         scratch_shapes=[
+            pltpu.VMEM(panels.shape, jnp.bfloat16),
+            pltpu.VMEM(tiles.shape, jnp.bfloat16),
             pltpu.VMEM((rows, width), jnp.float32),
             pltpu.VMEM((rows, width), jnp.float32),
+            pltpu.VMEM((3, rows, KG * BS), jnp.bfloat16),
+            pltpu.VMEM(tiles.shape, jnp.bfloat16),
+            pltpu.VMEM(panels.shape, jnp.bfloat16),
+            pltpu.SemaphoreType.DMA((2,)),
+            pltpu.SemaphoreType.DMA((tiles.shape[0],)),
+            pltpu.SemaphoreType.DMA((peers,)),
         ],
         compiler_params=pltpu.CompilerParams(vmem_limit_bytes=62 * 1024 * 1024),
         cost_estimate=pl.CostEstimate(

time: 213 us -> 212 us (level)
  no operation moved by 1% of the time
where the time goes in v7:
time: 212 us; the launch traced here: 211 us
  Pallas kernels  159 us (75%)
  waiting for transfers between devices  28.3 us (13%)
  between operations  14.1 us (7%)
  local copies, waits for them, and re-layouts  5.14 us (2%)
  other arithmetic  3.72 us (2%)
    pallas_call x1, Pallas kernels, scatter_rows(): pl.pallas_call(functools.partial(scatter_rows_kernel, n_row), out_shape=j...  79 us
    pallas_call x1, Pallas kernels, gather_rows(): pl.pallas_call(functools.partial(gather_rows_kernel, n_row), out_shape=ja...  56.7 us
    pallas_call x1, Pallas kernels, core(): pl.pallas_call(functools.partial(core_kernel, slots), out_shape=(jax.Shap...  23.7 us
    all_gather x1, waiting for transfers between devices, shards(): panels = lax.all_gather(jnp.stack([tokens, out_grad]), 'col', axis=0)  20.8 us
    reduce_scatter x1, waiting for transfers between devices, shards(): lax.psum_scatter(panel_part.reshape(peers * 2 * rows, chunk), 'col', scat...  7.54 us
  transfers between devices with their start and end apart: 2, of which 2 were waited for; matrix products, arithmetic and copies ran while one was open for 1% of the time, Pallas kernels for 64%

profile of v7, /device:TPU:64, one launch (start us, length us, event | category | flops | bytes accessed | tf_op | source)
XLA Modules:
  0.0 210.8 jit_solution(12236000394712304589)
XLA Ops:
  7.2 0.0 all-gather.3.cloned.1.call-start
  7.2 1.9 pad_maximum_fusion
  9.1 0.0 all-gather.3.cloned.1.call-update
  9.2 0.0 reduce-scatter.2.cloned.1.call-start
  9.2 1.8 pad_maximum_fusion.1.w_ref
  11.0 56.7 %shard_map.119.w_hbm = bf16[21,1024,128]{2,1,0:T(8,128)(2,1)} custom-call(bf16[21,64,128]{2,1,0:T(8,128)(2,1)} %pad_maximum_fusion.1.w_ref), custom_call_target="tpu_custom_call" | custom-call | bytes 5505024 | tf_op jit(solution)/shard_map/pallas_call | solution.py:95
  67.7 20.8 %all-gather.3.cloned.1.call-done = bf16[32,256,512]{2,1,0:T(8,128)(2,1)} async-done(((bf16[2,256,512]{2,1,0:T(8,128)(2,1)}), bf16[32,256,512]{2,1,0:T(8,128)(2,1)}) %all-gather.3.cloned.1.call-update) | async-done | bytes 8388624 | tf_op jit(solution)/shard_map/all_gather | solution.py:300
  88.5 23.7 %shard_map.120 = (bf16[16,2,256,512]{3,2,1,0:T(8,128)(2,1)}, bf16[21,1024,128]{2,1,0:T(8,128)(2,1)}) custom-call(s32[7,8]{1,0:T(8,128)} %gr_ref.1, s32[7,8]{1,0:T(8,128)} %ur_ref.1, s32[7,8]{1,0:T(8,128)} %dc_ref.1, bf16[16,2,256,512]{3,2,1,0:T(8,128)(2,1)} %bitcast.9, bf16[21,1024,128]{2,1,0:T(8,128)(2,1)} %shard_map.119.w_hbm), custom_call_target="tpu_custom_call" | custom-call | flops 4227858432 | bytes 27787264 | tf_op jit(solution)/shard_map/pallas_call | solution.py:271
  112.2 0.0 reduce-scatter.2.cloned.1.call-update
  112.2 0.0 copy-start
  112.2 2.6 %copy-done = bf16[21,1024,128]{2,1,0:T(8,128)(2,1)S(1)} copy-done((bf16[21,1024,128]{2,1,0:T(8,128)(2,1)S(1)}, bf16[21,1024,128]{2,1,0:T(8,128)(2,1)}, u32[]{:S(2)}) %copy-start) | copy-done | bytes 5505048
  114.8 79.0 %shard_map.121 = bf16[21,64,128]{2,1,0:T(8,128)(2,1)S(1)} custom-call(bf16[21,8,2,64,128]{4,3,2,1,0:T(8,128)(2,1)S(1)} %bitcast.5), custom_call_target="tpu_custom_call" | custom-call | flops 2752512 | bytes 11010048 | tf_op jit(solution)/shard_map/pallas_call | solution.py:167
  193.8 0.7 fusion.1
  194.5 7.5 %reduce-scatter.2.cloned.1.call-done = bf16[512,512]{1,0:T(8,128)(2,1)} async-done(((bf16[8192,512]{1,0:T(8,128)(2,1)}), bf16[512,512]{1,0:T(8,128)(2,1)}) %reduce-scatter.2.cloned.1.call-update) | async-done | bytes 524304 | tf_op jit(solution)/shard_map/reduce_scatter | solution.py:306
  202.1 1.9 fusion
Async XLA Ops:
  7.2 81.3 %all-gather.3.cloned.1.call-start = ((), (), s32[]{:S(2)}) async-start(), calls=%async_computation.2 | async-start | bytes 8912896 | tf_op jit(solution)/shard_map/all_gather | solution.py:300
  9.2 192.9 %reduce-scatter.2.cloned.1.call-start = ((), (), s32[]{:S(2)}) async-start(), calls=%async_computation.1 | async-start | bytes 8912896 | tf_op jit(solution)/shard_map/reduce_scatter | solution.py:306
  112.2 2.6 %copy-start = (bf16[21,1024,128]{2,1,0:T(8,128)(2,1)S(1)}, bf16[21,1024,128]{2,1,0:T(8,128)(2,1)}, u32[]{:S(2)}) copy-start(bf16[21,1024,128]{2,1,0:T(8,128)(2,1)} %get-tuple-element.8) | copy-start | bytes 16515076
Sparse Core Ops, SparseCore 0:
  10.4 77.9 all-gather.2
  112.3 89.6 reduce-scatter.1

commit v8 on v7

--- a/solution.py
+++ b/solution.py
@@ -15,8 +15,12 @@
 MESH = pl.DeviceIdType.MESH
 
 
-def gather_rows_kernel(n_row, w_ref, out_ref, lsem, psend, precv, rsend, rrecv, fsend, frecv):
+def gather_rows_kernel(
+    n_row, n_col, w_ref, g_ref, out_ref, gout_ref, lsem, psend, precv, rsend, rrecv, fsend, frecv,
+    glsem, csend, crecv,
+):
     me = lax.axis_index("row")
+    mc = lax.axis_index("col")
     n_chip = n_row // 2
     z = me // 2
     c = me % 2
@@ -30,7 +34,22 @@
     barrier = pltpu.get_barrier_semaphore()
     for peer in (partner, nxt, prv):
         pl.semaphore_signal(barrier, inc=1, device_id={"row": peer}, device_id_type=MESH)
-    pl.semaphore_wait(barrier, 3)
+    for d in range(1, n_col):
+        pl.semaphore_signal(
+            barrier, inc=1, device_id={"col": (mc + d) % n_col}, device_id_type=MESH
+        )
+    pl.semaphore_wait(barrier, 3 + n_col - 1)
+
+    glocal = pltpu.make_async_copy(g_ref, gout_ref.at[mc], glsem)
+    glocal.start()
+    col_sends = []
+    for d in range(1, n_col):
+        cp = pltpu.make_async_remote_copy(
+            src_ref=g_ref, dst_ref=gout_ref.at[mc], send_sem=csend.at[d - 1], recv_sem=crecv.at[d - 1],
+            device_id={"col": (mc + d) % n_col}, device_id_type=MESH,
+        )
+        cp.start()
+        col_sends.append(cp)
 
     def chip_tile(p):
         return out_ref.at[:, pl.ds(pl.multiple_of(p * tile, tile), tile), :]
@@ -84,19 +103,29 @@
             send_sem=fsend.at[s - 1], recv_sem=frecv.at[s - 1],
             device_id={"row": partner}, device_id_type=MESH,
         ).wait_recv()
-    for cp in sends + fwds:
+    for d in range(1, n_col):
+        src_col = (mc - d + n_col) % n_col
+        pltpu.make_async_remote_copy(
+            src_ref=g_ref, dst_ref=gout_ref.at[src_col], send_sem=csend.at[d - 1], recv_sem=crecv.at[d - 1],
+            device_id={"col": src_col}, device_id_type=MESH,
+        ).wait_recv()
+    glocal.wait()
+    for cp in sends + fwds + col_sends:
         cp.wait_send()
 
 
-def gather_rows(w, n_row):
+def gather_rows(w, g, n_row, n_col):
     slots, half, width = w.shape
     steps = n_row // 4
     any_spec = pl.BlockSpec(memory_space=pl.ANY)
     return pl.pallas_call(
-        functools.partial(gather_rows_kernel, n_row),
-        out_shape=jax.ShapeDtypeStruct((slots, half * n_row, width), w.dtype),
-        in_specs=[any_spec],
-        out_specs=any_spec,
+        functools.partial(gather_rows_kernel, n_row, n_col),
+        out_shape=(
+            jax.ShapeDtypeStruct((slots, half * n_row, width), w.dtype),
+            jax.ShapeDtypeStruct((n_col,) + g.shape, g.dtype),
+        ),
+        in_specs=[any_spec, any_spec],
+        out_specs=(any_spec, any_spec),
         scratch_shapes=[
             pltpu.SemaphoreType.DMA(()),
             pltpu.SemaphoreType.DMA(()),
@@ -105,10 +134,15 @@
             pltpu.SemaphoreType.DMA((steps,)),
             pltpu.SemaphoreType.DMA((steps - 1,)),
             pltpu.SemaphoreType.DMA((steps - 1,)),
+            pltpu.SemaphoreType.DMA(()),
+            pltpu.SemaphoreType.DMA((n_col - 1,)),
+            pltpu.SemaphoreType.DMA((n_col - 1,)),
         ],
         compiler_params=pltpu.CompilerParams(collective_id=0, has_side_effects=True),
-        cost_estimate=pl.CostEstimate(flops=0, transcendentals=0, bytes_accessed=2 * w.size * n_row),
-    )(w)
+        cost_estimate=pl.CostEstimate(
+            flops=0, transcendentals=0, bytes_accessed=2 * w.size * n_row + 2 * g.size * n_col
+        ),
+    )(w, g)
 
 
 def scatter_rows_kernel(n_row, x_ref, out_ref, part_buf, send_buf, recv_buf, psend, precv, rsend, rrecv):
@@ -188,7 +222,7 @@
 
 
 def core_kernel(
-    slots, gr_ref, ur_ref, dc_ref, p_hbm, w_hbm, panel_hbm, tiles_hbm,
+    slots, gr_ref, ur_ref, dc_ref, x_hbm, g_hbm, w_hbm, panel_hbm, tiles_hbm,
     p_buf, w_buf, out_acc, in_acc, gath, tstage, pstage, isem, tsem, psem,
 ):
     f32 = jnp.float32
@@ -199,12 +233,15 @@
     nt = (((1,), (1,)), ((), ()))
     cp_w = pltpu.make_async_copy(w_hbm, w_buf, isem.at[0])
     cp_w.start()
-    cp_p = pltpu.make_async_copy(p_hbm, p_buf, isem.at[1])
-    cp_p.start()
+    cp_x = pltpu.make_async_copy(x_hbm, p_buf.at[:, 0], isem.at[1])
+    cp_x.start()
+    cp_g = pltpu.make_async_copy(g_hbm, p_buf.at[:, 1], isem.at[2])
+    cp_g.start()
     out_acc[...] = jnp.zeros_like(out_acc)
     in_acc[...] = jnp.zeros_like(in_acc)
     cp_w.wait()
-    cp_p.wait()
+    cp_x.wait()
+    cp_g.wait()
 
     def col(b):
         return pl.ds(pl.multiple_of(b * BS, BS), BS)
@@ -260,21 +297,22 @@
         cp.wait()
 
 
-def core(panels, tiles, gate_rows, up_rows, down_columns):
+def core(x_panel, g_panel, tiles, gate_rows, up_rows, down_columns):
     slots = gate_rows.shape[0]
-    peers, _, rows, chunk = panels.shape
+    peers, rows, chunk = x_panel.shape
+    panels = jax.ShapeDtypeStruct((peers, 2, rows, chunk), x_panel.dtype)
     width = peers * chunk
     smem = pl.BlockSpec(memory_space=pltpu.SMEM)
     any_spec = pl.BlockSpec(memory_space=pl.ANY)
     flops = 2 * rows * BS * BS * slots * KG * 9
-    nbytes = 2 * (2 * panels.size + 2 * tiles.size)
+    nbytes = 2 * (4 * x_panel.size + 2 * tiles.size)
     return pl.pallas_call(
         functools.partial(core_kernel, slots),
         out_shape=(
             jax.ShapeDtypeStruct(panels.shape, jnp.bfloat16),
             jax.ShapeDtypeStruct(tiles.shape, jnp.bfloat16),
         ),
-        in_specs=[smem, smem, smem, any_spec, any_spec],
+        in_specs=[smem, smem, smem, any_spec, any_spec, any_spec],
         out_specs=(any_spec, any_spec),
         scratch_shapes=[
             pltpu.VMEM(panels.shape, jnp.bfloat16),
@@ -284,7 +322,7 @@
             pltpu.VMEM((3, rows, KG * BS), jnp.bfloat16),
             pltpu.VMEM(tiles.shape, jnp.bfloat16),
             pltpu.VMEM(panels.shape, jnp.bfloat16),
-            pltpu.SemaphoreType.DMA((2,)),
+            pltpu.SemaphoreType.DMA((3,)),
             pltpu.SemaphoreType.DMA((tiles.shape[0],)),
             pltpu.SemaphoreType.DMA((peers,)),
         ],
@@ -292,15 +330,18 @@
         cost_estimate=pl.CostEstimate(
             flops=flops, transcendentals=rows * BS * slots, bytes_accessed=nbytes
         ),
-    )(gate_rows, up_rows, down_columns, panels, tiles)
+    )(gate_rows, up_rows, down_columns, x_panel, g_panel, tiles)
 
 
 def shards(tokens, out_grad, gate_weight, up_weight, down_weight, gate_rows, up_rows, down_columns):
     owned_slots = gate_weight.shape[0]
-    panels = lax.all_gather(jnp.stack([tokens, out_grad]), "col", axis=0)
+    x_panel = lax.all_gather(tokens, "col", axis=0)
     n_row = lax.axis_size("row")
-    tiles = gather_rows(jnp.concatenate([gate_weight, up_weight, down_weight], axis=0), n_row)
-    panel_part, tile_part = core(panels, tiles, gate_rows, up_rows, down_columns)
+    n_col = lax.axis_size("col")
+    tiles, g_panel = gather_rows(
+        jnp.concatenate([gate_weight, up_weight, down_weight], axis=0), out_grad, n_row, n_col
+    )
+    panel_part, tile_part = core(x_panel, g_panel, tiles, gate_rows, up_rows, down_columns)
     tile_sums = scatter_rows(tile_part, n_row)
     peers, _, rows, chunk = panel_part.shape
     panel_sums = lax.psum_scatter(

time: 212 us -> 250 us (1.18)
  Pallas kernels: 159 us -> 180 us
  waiting for transfers between devices: 28.3 us -> 47.6 us
    pallas_call x1, Pallas kernels: 56.7 us -> 77.3 us  [gather_rows(): pl.pallas_call(functools.partial(gather_rows_kernel, n_row, n_col), out_s...]
    all_gather x1, waiting for transfers between devices: 20.8 us -> 32.5 us  [shards(): x_panel = lax.all_gather(tokens, 'col', axis=0)]
    reduce_scatter x1, waiting for transfers between devices: 7.54 us -> 14.4 us  [shards(): lax.psum_scatter(panel_part.reshape(peers * 2 * rows, chunk), 'col', scat...]
  transfers between devices with their start and end apart: 2 -> 2, of which waited for: 2 -> 2; matrix products, arithmetic and copies ran while one was open for 1% -> 1% of each run, Pallas kernels for 64% -> 63%
where the time goes in v8:
time: 250 us; the launch traced here: 249 us
  Pallas kernels  180 us (72%)
  waiting for transfers between devices  47.6 us (19%)
  between operations  14.1 us (6%)
  local copies, waits for them, and re-layouts  5.14 us (2%)
    pallas_call x1, Pallas kernels, scatter_rows(): pl.pallas_call(functools.partial(scatter_rows_kernel, n_row), out_shape=j...  79 us
    pallas_call x1, Pallas kernels, gather_rows(): pl.pallas_call(functools.partial(gather_rows_kernel, n_row, n_col), out_s...  77.3 us
    all_gather x1, waiting for transfers between devices, shards(): x_panel = lax.all_gather(tokens, 'col', axis=0)  32.5 us
    pallas_call x1, Pallas kernels, core(): pl.pallas_call(functools.partial(core_kernel, slots), out_shape=(jax.Shap...  23.7 us
    reduce_scatter x1, waiting for transfers between devices, shards(): lax.psum_scatter(panel_part.reshape(peers * 2 * rows, chunk), 'col', scat...  14.4 us
  transfers between devices with their start and end apart: 2, of which 2 were waited for; matrix products, arithmetic and copies ran while one was open for 1% of the time, Pallas kernels for 63%

profile of v8, /device:TPU:64, one launch (start us, length us, event | category | flops | bytes accessed | tf_op | source)
XLA Modules:
  0.0 248.7 jit_solution(3104924322428735086)
XLA Ops:
  7.2 0.0 all-gather.3.cloned.1.call-start
  7.2 0.7 all-gather.3.cloned.1.call-update
  7.9 0.0 reduce-scatter.2.cloned.1.call-start
  7.9 1.8 pad_maximum_fusion.w_ref
  9.7 77.3 %shard_map.119 = (bf16[21,1024,128]{2,1,0:T(8,128)(2,1)}, bf16[16,256,512]{2,1,0:T(8,128)(2,1)}) custom-call(bf16[21,64,128]{2,1,0:T(8,128)(2,1)} %pad_maximum_fusion.w_ref, bf16[256,512]{1,0:T(8,128)(2,1)} %g_ref.1), custom_call_target="tpu_custom_call" | custom-call | bytes 9699328 | tf_op jit(solution)/shard_map/pallas_call | solution.py:121
  87.1 32.5 %all-gather.3.cloned.1.call-done = bf16[4096,512]{1,0:T(8,128)(2,1)} async-done(((bf16[256,512]{1,0:T(8,128)(2,1)}), bf16[4096,512]{1,0:T(8,128)(2,1)}) %all-gather.3.cloned.1.call-update) | async-done | bytes 4194320 | tf_op jit(solution)/shard_map/all_gather | solution.py:338
  119.5 23.7 %shard_map.120 = (bf16[16,2,256,512]{3,2,1,0:T(8,128)(2,1)}, bf16[21,1024,128]{2,1,0:T(8,128)(2,1)}) custom-call(s32[7,8]{1,0:T(8,128)} %gr_ref.1, s32[7,8]{1,0:T(8,128)} %ur_ref.1, s32[7,8]{1,0:T(8,128)} %dc_ref.1, bf16[16,256,512]{2,1,0:T(8,128)(2,1)} %bitcast.5, bf16[16,256,512]{2,1,0:T(8,128)(2,1)} %get-tuple-element.9.g_hbm, ...), custom_call_target="tpu_custom_call" | custom-call | flops 4227858432 | bytes 27787264 | tf_op jit(solution)/shard_map/pallas_call | solution.py:309
  143.3 0.0 reduce-scatter.2.cloned.1.call-update
  143.3 0.0 copy-start
  143.3 2.6 %copy-done = bf16[21,1024,128]{2,1,0:T(8,128)(2,1)S(1)} copy-done((bf16[21,1024,128]{2,1,0:T(8,128)(2,1)S(1)}, bf16[21,1024,128]{2,1,0:T(8,128)(2,1)}, u32[]{:S(2)}) %copy-start) | copy-done | bytes 5505048
  145.8 79.0 %shard_map.121 = bf16[21,64,128]{2,1,0:T(8,128)(2,1)S(1)} custom-call(bf16[21,8,2,64,128]{4,3,2,1,0:T(8,128)(2,1)S(1)} %bitcast.3), custom_call_target="tpu_custom_call" | custom-call | flops 2752512 | bytes 11010048 | tf_op jit(solution)/shard_map/pallas_call | solution.py:201
  224.9 0.7 fusion.1
  225.6 14.4 %reduce-scatter.2.cloned.1.call-done = bf16[512,512]{1,0:T(8,128)(2,1)} async-done(((bf16[8192,512]{1,0:T(8,128)(2,1)}), bf16[512,512]{1,0:T(8,128)(2,1)}) %reduce-scatter.2.cloned.1.call-update) | async-done | bytes 524304 | tf_op jit(solution)/shard_map/reduce_scatter | solution.py:347
  240.0 1.9 fusion
Async XLA Ops:
  7.2 112.4 %all-gather.3.cloned.1.call-start = ((), (), s32[]{:S(2)}) async-start(), calls=%async_computation.2 | async-start | bytes 4456448 | tf_op jit(solution)/shard_map/all_gather | solution.py:338
  7.9 232.1 %reduce-scatter.2.cloned.1.call-start = ((), (), s32[]{:S(2)}) async-start(), calls=%async_computation.1 | async-start | bytes 8912896 | tf_op jit(solution)/shard_map/reduce_scatter | solution.py:347
  143.3 2.6 %copy-start = (bf16[21,1024,128]{2,1,0:T(8,128)(2,1)S(1)}, bf16[21,1024,128]{2,1,0:T(8,128)(2,1)}, u32[]{:S(2)}) copy-start(bf16[21,1024,128]{2,1,0:T(8,128)(2,1)} %get-tuple-element.12) | copy-start | bytes 16515076
Sparse Core Ops, SparseCore 0:
  10.4 109.0 all-gather.2
  143.4 96.5 reduce-scatter.1

commit v9 on v7

--- a/solution.py
+++ b/solution.py
@@ -213,17 +213,18 @@
         return p_buf[b // per, which, :, pl.ds(pl.multiple_of((b % per) * BS, BS), BS)]
 
     def body(f, carry):
+        gbuf = gath.at[f % 2]
         for k in range(KG):
             ks = pl.ds(k * BS, BS)
-            gath[0, :, ks] = block(0, gr_ref[f, k])
-            gath[1, :, ks] = block(0, ur_ref[f, k])
-            gath[2, :, ks] = block(1, dc_ref[f, k])
+            gbuf[0, :, ks] = block(0, gr_ref[f, k])
+            gbuf[1, :, ks] = block(0, ur_ref[f, k])
+            gbuf[2, :, ks] = block(1, dc_ref[f, k])
         gw = w_buf[f]
         uw = w_buf[slots + f]
         dw = w_buf[2 * slots + f]
-        gate = jnp.dot(gath[0], gw, preferred_element_type=f32)
-        up = jnp.dot(gath[1], uw, preferred_element_type=f32)
-        hg = jnp.dot(gath[2], dw, preferred_element_type=f32)
+        gate = jnp.dot(gbuf[0], gw, preferred_element_type=f32)
+        up = jnp.dot(gbuf[1], uw, preferred_element_type=f32)
+        hg = jnp.dot(gbuf[2], dw, preferred_element_type=f32)
         sg = 1.0 / (1.0 + jnp.exp(-gate))
         silu = gate * sg
         hidden = (silu * up).astype(bf16)
@@ -237,15 +238,15 @@
             out_acc[:, col(dc_ref[f, k])] += po[:, ks]
             in_acc[:, col(gr_ref[f, k])] += pg[:, ks]
             in_acc[:, col(ur_ref[f, k])] += pu[:, ks]
-        tstage[f] = lax.dot_general(gath[0], gg, tn, preferred_element_type=f32).astype(bf16)
-        tstage[slots + f] = lax.dot_general(gath[1], ug, tn, preferred_element_type=f32).astype(bf16)
-        tstage[2 * slots + f] = lax.dot_general(gath[2], hidden, tn, preferred_element_type=f32).astype(bf16)
+        tstage[f] = lax.dot_general(gbuf[0], gg, tn, preferred_element_type=f32).astype(bf16)
+        tstage[slots + f] = lax.dot_general(gbuf[1], ug, tn, preferred_element_type=f32).astype(bf16)
+        tstage[2 * slots + f] = lax.dot_general(gbuf[2], hidden, tn, preferred_element_type=f32).astype(bf16)
         for part in range(3):
             s = part * slots + f
             pltpu.make_async_copy(tstage.at[s], tiles_hbm.at[s], tsem.at[s]).start()
         return carry
 
-    lax.fori_loop(0, slots, body, 0)
+    lax.fori_loop(0, slots, body, 0, unroll=True)
     outs = []
     for j in range(peers):
         cs = pl.ds(j * chunk, chunk)
@@ -281,7 +282,7 @@
             pltpu.VMEM(tiles.shape, jnp.bfloat16),
             pltpu.VMEM((rows, width), jnp.float32),
             pltpu.VMEM((rows, width), jnp.float32),
-            pltpu.VMEM((3, rows, KG * BS), jnp.bfloat16),
+            pltpu.VMEM((2, 3, rows, KG * BS), jnp.bfloat16),
             pltpu.VMEM(tiles.shape, jnp.bfloat16),
             pltpu.VMEM(panels.shape, jnp.bfloat16),
             pltpu.SemaphoreType.DMA((2,)),

time: 212 us -> 211 us (level)
  transfers between devices with their start and end apart: 2 -> 2, of which waited for: 2 -> 2; matrix products, arithmetic and copies ran while one was open for 1% -> 1% of each run, Pallas kernels for 64% -> 65%
where the time goes in v9:
time: 211 us; the launch traced here: 210 us
  Pallas kernels  159 us (75%)
  waiting for transfers between devices  28.2 us (13%)
  between operations  14.1 us (7%)
  local copies, waits for them, and re-layouts  5.14 us (2%)
  other arithmetic  3.72 us (2%)
    pallas_call x1, Pallas kernels, scatter_rows(): pl.pallas_call(functools.partial(scatter_rows_kernel, n_row), out_shape=j...  79 us
    pallas_call x1, Pallas kernels, gather_rows(): pl.pallas_call(functools.partial(gather_rows_kernel, n_row), out_shape=ja...  56.7 us
    pallas_call x1, Pallas kernels, core(): pl.pallas_call(functools.partial(core_kernel, slots), out_shape=(jax.Shap...  23.4 us
    all_gather x1, waiting for transfers between devices, shards(): panels = lax.all_gather(jnp.stack([tokens, out_grad]), 'col', axis=0)  20.8 us
    reduce_scatter x1, waiting for transfers between devices, shards(): lax.psum_scatter(panel_part.reshape(peers * 2 * rows, chunk), 'col', scat...  7.37 us
  transfers between devices with their start and end apart: 2, of which 2 were waited for; matrix products, arithmetic and copies ran while one was open for 1% of the time, Pallas kernels for 65%

profile of v9, /device:TPU:64, one launch (start us, length us, event | category | flops | bytes accessed | tf_op | source)
XLA Modules:
  0.0 210.3 jit_solution(1206040156205513754)
XLA Ops:
  7.2 0.0 all-gather.3.cloned.1.call-start
  7.2 1.9 pad_maximum_fusion
  9.1 0.0 all-gather.3.cloned.1.call-update
  9.2 0.0 reduce-scatter.2.cloned.1.call-start
  9.2 1.8 pad_maximum_fusion.1.w_ref
  11.0 56.7 %shard_map.119.w_hbm = bf16[21,1024,128]{2,1,0:T(8,128)(2,1)} custom-call(bf16[21,64,128]{2,1,0:T(8,128)(2,1)} %pad_maximum_fusion.1.w_ref), custom_call_target="tpu_custom_call" | custom-call | bytes 5505024 | tf_op jit(solution)/shard_map/pallas_call | solution.py:95
  67.7 20.8 %all-gather.3.cloned.1.call-done = bf16[32,256,512]{2,1,0:T(8,128)(2,1)} async-done(((bf16[2,256,512]{2,1,0:T(8,128)(2,1)}), bf16[32,256,512]{2,1,0:T(8,128)(2,1)}) %all-gather.3.cloned.1.call-update) | async-done | bytes 8388624 | tf_op jit(solution)/shard_map/all_gather | solution.py:301
  88.5 23.4 %shard_map.120 = (bf16[16,2,256,512]{3,2,1,0:T(8,128)(2,1)}, bf16[21,1024,128]{2,1,0:T(8,128)(2,1)}) custom-call(s32[7,8]{1,0:T(8,128)} %gr_ref.1, s32[7,8]{1,0:T(8,128)} %ur_ref.1, s32[7,8]{1,0:T(8,128)} %dc_ref.1, bf16[16,2,256,512]{3,2,1,0:T(8,128)(2,1)} %bitcast.9, bf16[21,1024,128]{2,1,0:T(8,128)(2,1)} %shard_map.119.w_hbm), custom_call_target="tpu_custom_call" | custom-call | flops 4227858432 | bytes 27787264 | tf_op jit(solution)/shard_map/pallas_call | solution.py:272
  111.9 0.0 reduce-scatter.2.cloned.1.call-update
  111.9 0.0 copy-start
  111.9 2.6 %copy-done = bf16[21,1024,128]{2,1,0:T(8,128)(2,1)S(1)} copy-done((bf16[21,1024,128]{2,1,0:T(8,128)(2,1)S(1)}, bf16[21,1024,128]{2,1,0:T(8,128)(2,1)}, u32[]{:S(2)}) %copy-start) | copy-done | bytes 5505048
  114.5 79.0 %shard_map.121 = bf16[21,64,128]{2,1,0:T(8,128)(2,1)S(1)} custom-call(bf16[21,8,2,64,128]{4,3,2,1,0:T(8,128)(2,1)S(1)} %bitcast.5), custom_call_target="tpu_custom_call" | custom-call | flops 2752512 | bytes 11010048 | tf_op jit(solution)/shard_map/pallas_call | solution.py:167
  193.5 0.7 fusion.1
  194.2 7.4 %reduce-scatter.2.cloned.1.call-done = bf16[512,512]{1,0:T(8,128)(2,1)} async-done(((bf16[8192,512]{1,0:T(8,128)(2,1)}), bf16[512,512]{1,0:T(8,128)(2,1)}) %reduce-scatter.2.cloned.1.call-update) | async-done | bytes 524304 | tf_op jit(solution)/shard_map/reduce_scatter | solution.py:307
  201.6 1.9 fusion
Async XLA Ops:
  7.2 81.3 %all-gather.3.cloned.1.call-start = ((), (), s32[]{:S(2)}) async-start(), calls=%async_computation.2 | async-start | bytes 8912896 | tf_op jit(solution)/shard_map/all_gather | solution.py:301
  9.2 192.5 %reduce-scatter.2.cloned.1.call-start = ((), (), s32[]{:S(2)}) async-start(), calls=%async_computation.1 | async-start | bytes 8912896 | tf_op jit(solution)/shard_map/reduce_scatter | solution.py:307
  111.9 2.6 %copy-start = (bf16[21,1024,128]{2,1,0:T(8,128)(2,1)S(1)}, bf16[21,1024,128]{2,1,0:T(8,128)(2,1)}, u32[]{:S(2)}) copy-start(bf16[21,1024,128]{2,1,0:T(8,128)(2,1)} %get-tuple-element.8) | copy-start | bytes 16515076
Sparse Core Ops, SparseCore 0:
  10.4 77.9 all-gather.2
  112.0 89.5 reduce-scatter.1

commit v10 on v7

--- a/solution.py
+++ b/solution.py
@@ -188,14 +188,13 @@
 
 
 def core_kernel(
-    slots, gr_ref, ur_ref, dc_ref, p_hbm, w_hbm, panel_hbm, tiles_hbm,
-    p_buf, w_buf, out_acc, in_acc, gath, tstage, pstage, isem, tsem, psem,
+    slots, gr_ref, ur_ref, dc_ref, p_hbm, w_hbm, panel_hbm, acts_ref,
+    p_buf, w_buf, out_acc, in_acc, gath, pstage, isem, psem,
 ):
     f32 = jnp.float32
     bf16 = jnp.bfloat16
     peers, _, rows, chunk = p_buf.shape
     per = chunk // BS
-    tn = (((0,), (0,)), ((), ()))
     nt = (((1,), (1,)), ((), ()))
     cp_w = pltpu.make_async_copy(w_hbm, w_buf, isem.at[0])
     cp_w.start()
@@ -229,6 +228,9 @@
         hidden = (silu * up).astype(bf16)
         gg = (hg * up * sg * (1.0 + gate * (1.0 - sg))).astype(bf16)
         ug = (hg * silu).astype(bf16)
+        acts_ref[0, f] = hidden
+        acts_ref[1, f] = gg
+        acts_ref[2, f] = ug
         po = lax.dot_general(hidden, dw, nt, preferred_element_type=f32)
         pg = lax.dot_general(gg, gw, nt, preferred_element_type=f32)
         pu = lax.dot_general(ug, uw, nt, preferred_element_type=f32)
@@ -237,12 +239,6 @@
             out_acc[:, col(dc_ref[f, k])] += po[:, ks]
             in_acc[:, col(gr_ref[f, k])] += pg[:, ks]
             in_acc[:, col(ur_ref[f, k])] += pu[:, ks]
-        tstage[f] = lax.dot_general(gath[0], gg, tn, preferred_element_type=f32).astype(bf16)
-        tstage[slots + f] = lax.dot_general(gath[1], ug, tn, preferred_element_type=f32).astype(bf16)
-        tstage[2 * slots + f] = lax.dot_general(gath[2], hidden, tn, preferred_element_type=f32).astype(bf16)
-        for part in range(3):
-            s = part * slots + f
-            pltpu.make_async_copy(tstage.at[s], tiles_hbm.at[s], tsem.at[s]).start()
         return carry
 
     lax.fori_loop(0, slots, body, 0)
@@ -254,10 +250,40 @@
         cp = pltpu.make_async_copy(pstage.at[j], panel_hbm.at[j], psem.at[j])
         cp.start()
         outs.append(cp)
+    for cp in outs:
+        cp.wait()
+
+
+def tile_kernel(slots, gr_ref, ur_ref, dc_ref, p_hbm, acts_ref, tiles_hbm, p_buf, gath, tstage, isem, tsem):
+    f32 = jnp.float32
+    bf16 = jnp.bfloat16
+    peers, _, rows, chunk = p_buf.shape
+    per = chunk // BS
+    tn = (((0,), (0,)), ((), ()))
+    cp_p = pltpu.make_async_copy(p_hbm, p_buf, isem)
+    cp_p.start()
+    cp_p.wait()
+
+    def block(which, b):
+        return p_buf[b // per, which, :, pl.ds(pl.multiple_of((b % per) * BS, BS), BS)]
+
+    def body(f, carry):
+        for k in range(KG):
+            ks = pl.ds(k * BS, BS)
+            gath[0, :, ks] = block(0, gr_ref[f, k])
+            gath[1, :, ks] = block(0, ur_ref[f, k])
+            gath[2, :, ks] = block(1, dc_ref[f, k])
+        tstage[f] = lax.dot_general(gath[0], acts_ref[1, f], tn, preferred_element_type=f32).astype(bf16)
+        tstage[slots + f] = lax.dot_general(gath[1], acts_ref[2, f], tn, preferred_element_type=f32).astype(bf16)
+        tstage[2 * slots + f] = lax.dot_general(gath[2], acts_ref[0, f], tn, preferred_element_type=f32).astype(bf16)
+        for part in range(3):
+            s = part * slots + f
+            pltpu.make_async_copy(tstage.at[s], tiles_hbm.at[s], tsem.at[s]).start()
+        return carry
+
+    lax.fori_loop(0, slots, body, 0)
     for s in range(3 * slots):
         pltpu.make_async_copy(tstage.at[s], tiles_hbm.at[s], tsem.at[s]).wait()
-    for cp in outs:
-        cp.wait()
 
 
 def core(panels, tiles, gate_rows, up_rows, down_columns):
@@ -265,34 +291,52 @@
     peers, _, rows, chunk = panels.shape
     width = peers * chunk
     smem = pl.BlockSpec(memory_space=pltpu.SMEM)
+    vmem = pl.BlockSpec(memory_space=pltpu.VMEM)
     any_spec = pl.BlockSpec(memory_space=pl.ANY)
-    flops = 2 * rows * BS * BS * slots * KG * 9
-    nbytes = 2 * (2 * panels.size + 2 * tiles.size)
-    return pl.pallas_call(
+    dot_flops = 2 * rows * BS * BS * slots * KG
+    panel_part, acts = pl.pallas_call(
         functools.partial(core_kernel, slots),
         out_shape=(
             jax.ShapeDtypeStruct(panels.shape, jnp.bfloat16),
-            jax.ShapeDtypeStruct(tiles.shape, jnp.bfloat16),
+            jax.ShapeDtypeStruct((3, slots, rows, BS), jnp.bfloat16),
         ),
         in_specs=[smem, smem, smem, any_spec, any_spec],
-        out_specs=(any_spec, any_spec),
+        out_specs=(any_spec, vmem),
         scratch_shapes=[
             pltpu.VMEM(panels.shape, jnp.bfloat16),
             pltpu.VMEM(tiles.shape, jnp.bfloat16),
             pltpu.VMEM((rows, width), jnp.float32),
             pltpu.VMEM((rows, width), jnp.float32),
             pltpu.VMEM((3, rows, KG * BS), jnp.bfloat16),
-            pltpu.VMEM(tiles.shape, jnp.bfloat16),
             pltpu.VMEM(panels.shape, jnp.bfloat16),
             pltpu.SemaphoreType.DMA((2,)),
-            pltpu.SemaphoreType.DMA((tiles.shape[0],)),
             pltpu.SemaphoreType.DMA((peers,)),
         ],
         compiler_params=pltpu.CompilerParams(vmem_limit_bytes=62 * 1024 * 1024),
         cost_estimate=pl.CostEstimate(
-            flops=flops, transcendentals=rows * BS * slots, bytes_accessed=nbytes
+            flops=6 * dot_flops, transcendentals=rows * BS * slots,
+            bytes_accessed=2 * (2 * panels.size + tiles.size),
         ),
     )(gate_rows, up_rows, down_columns, panels, tiles)
+    tile_part = pl.pallas_call(
+        functools.partial(tile_kernel, slots),
+        out_shape=jax.ShapeDtypeStruct(tiles.shape, jnp.bfloat16),
+        in_specs=[smem, smem, smem, any_spec, vmem],
+        out_specs=any_spec,
+        scratch_shapes=[
+            pltpu.VMEM(panels.shape, jnp.bfloat16),
+            pltpu.VMEM((3, rows, KG * BS), jnp.bfloat16),
+            pltpu.VMEM(tiles.shape, jnp.bfloat16),
+            pltpu.SemaphoreType.DMA(()),
+            pltpu.SemaphoreType.DMA((tiles.shape[0],)),
+        ],
+        compiler_params=pltpu.CompilerParams(vmem_limit_bytes=40 * 1024 * 1024),
+        cost_estimate=pl.CostEstimate(
+            flops=3 * dot_flops, transcendentals=0,
+            bytes_accessed=2 * (panels.size + tiles.size),
+        ),
+    )(gate_rows, up_rows, down_columns, panels, acts)
+    return panel_part, tile_part
 
 
 def shards(tokens, out_grad, gate_weight, up_weight, down_weight, gate_rows, up_rows, down_columns):

time: 212 us -> 211 us (level)
  Pallas kernels: 159 us -> 168 us
  waiting for transfers between devices: 28.3 us -> 20.8 us
    pallas_call x0 -> x1, Pallas kernels: none -> 10.7 us  [core(): pl.pallas_call(functools.partial(tile_kernel, slots), out_shape=jax.Shape...]
    reduce_scatter x1, waiting for transfers between devices: 7.54 us -> 0.01 us  [shards(): lax.psum_scatter(panel_part.reshape(peers * 2 * rows, chunk), 'col', scat...]
    pallas_call x1, Pallas kernels: 23.7 us -> 21.4 us  [core(): pl.pallas_call(functools.partial(core_kernel, slots), out_shape=(jax.Shap...]
  transfers between devices with their start and end apart: 2 -> 2, of which waited for: 2 -> 1; matrix products, arithmetic and copies ran while one was open for 1% -> 1% of each run, Pallas kernels for 64% -> 70%
where the time goes in v10:
time: 211 us
  Pallas kernels  168 us (80%)
  waiting for transfers between devices  20.8 us (10%)
  between operations  14.1 us (7%)
  local copies, waits for them, and re-layouts  3.87 us (2%)
  other arithmetic  3.75 us (2%)
    pallas_call x1, Pallas kernels, scatter_rows(): pl.pallas_call(functools.partial(scatter_rows_kernel, n_row), out_shape=j...  79.2 us
    pallas_call x1, Pallas kernels, gather_rows(): pl.pallas_call(functools.partial(gather_rows_kernel, n_row), out_shape=ja...  56.7 us
    pallas_call x1, Pallas kernels, core(): pl.pallas_call(functools.partial(core_kernel, slots), out_shape=(jax.Shap...  21.4 us
    all_gather x1, waiting for transfers between devices, shards(): panels = lax.all_gather(jnp.stack([tokens, out_grad]), 'col', axis=0)  20.7 us
    pallas_call x1, Pallas kernels, core(): pl.pallas_call(functools.partial(tile_kernel, slots), out_shape=jax.Shape...  10.7 us
  transfers between devices with their start and end apart: 2, of which 1 were waited for; matrix products, arithmetic and copies ran while one was open for 1% of the time, Pallas kernels for 70%

profile of v10, /device:TPU:64, one launch (start us, length us, event | category | flops | bytes accessed | tf_op | source)
XLA Modules:
  0.0 210.5 jit_solution(14002062942815667886)
XLA Ops:
  7.2 0.0 all-gather.3.cloned.1.call-start
  7.2 1.9 pad_maximum_fusion
  9.1 0.0 all-gather.3.cloned.1.call-update
  9.2 0.0 reduce-scatter.2.cloned.1.call-start
  9.2 1.8 pad_maximum_fusion.1.w_ref
  11.0 56.7 %shard_map.119.w_hbm = bf16[21,1024,128]{2,1,0:T(8,128)(2,1)} custom-call(bf16[21,64,128]{2,1,0:T(8,128)(2,1)} %pad_maximum_fusion.1.w_ref), custom_call_target="tpu_custom_call" | custom-call | bytes 5505024 | tf_op jit(solution)/shard_map/pallas_call | solution.py:95
  67.7 20.7 %all-gather.3.cloned.1.call-done = bf16[32,256,512]{2,1,0:T(8,128)(2,1)} async-done(((bf16[2,256,512]{2,1,0:T(8,128)(2,1)}), bf16[32,256,512]{2,1,0:T(8,128)(2,1)}) %all-gather.3.cloned.1.call-update) | async-done | bytes 8388624 | tf_op jit(solution)/shard_map/all_gather | solution.py:344
  88.5 21.4 %shard_map.120 = (bf16[16,2,256,512]{3,2,1,0:T(8,128)(2,1)}, bf16[3,7,256,128]{3,2,1,0:T(8,128)(2,1)}) custom-call(s32[7,8]{1,0:T(8,128)} %gr_ref.3, s32[7,8]{1,0:T(8,128)} %ur_ref.3, s32[7,8]{1,0:T(8,128)} %dc_ref.3, bf16[16,2,256,512]{3,2,1,0:T(8,128)(2,1)} %bitcast.6, bf16[21,1024,128]{2,1,0:T(8,128)(2,1)} %shard_map.119.w_hbm), custom_call_target="tpu_custom_call" | custom-call | flops 2818572288 | bytes 22282240 | tf_op jit(solution)/shard_map/pallas_call | solution.py:297
  109.9 0.0 copy-start
  109.9 0.0 copy-start.1
  109.9 0.0 copy-start.2
  109.9 0.0 copy-start.3
  110.0 0.0 reduce-scatter.2.cloned.1.call-update
  110.0 1.3 copy-done
  111.2 0.0 copy-done.1
  111.3 0.0 copy-done.2
  111.3 0.0 copy-done.3
  111.3 10.7 %shard_map.121 = bf16[21,1024,128]{2,1,0:T(8,128)(2,1)S(1)} custom-call(s32[7,8]{1,0:T(8,128)S(1)} %copy-done.1, s32[7,8]{1,0:T(8,128)S(1)} %copy-done.2, s32[7,8]{1,0:T(8,128)S(1)} %copy-done.3, bf16[16,2,256,512]{3,2,1,0:T(8,128)(2,1)} %bitcast.7, bf16[3,7,256,128]{3,2,1,0:T(8,128)(2,1)S(1)} %copy-done), custom_call_target="tpu_custom_call" | custom-call | flops 1409286144 | bytes 13893632 | tf_op jit(solution)/shard_map/pallas_call | solution.py:321
  121.9 79.2 %shard_map.122 = bf16[21,64,128]{2,1,0:T(8,128)(2,1)S(1)} custom-call(bf16[21,8,2,64,128]{4,3,2,1,0:T(8,128)(2,1)S(1)} %bitcast.5), custom_call_target="tpu_custom_call" | custom-call | flops 2752512 | bytes 11010048 | tf_op jit(solution)/shard_map/pallas_call | solution.py:167
  201.1 0.7 fusion.1
  201.8 0.0 reduce-scatter.2.cloned.1.call-done
  201.8 1.9 fusion
Async XLA Ops:
  7.2 81.3 %all-gather.3.cloned.1.call-start = ((), (), s32[]{:S(2)}) async-start(), calls=%async_computation.2 | async-start | bytes 8912896 | tf_op jit(solution)/shard_map/all_gather | solution.py:344
  9.2 192.7 %reduce-scatter.2.cloned.1.call-start = ((), (), s32[]{:S(2)}) async-start(), calls=%async_computation.1 | async-start | bytes 8912896 | tf_op jit(solution)/shard_map/reduce_scatter | solution.py:350
  109.9 1.3 copy-start
  109.9 1.3 copy-start.1
  109.9 1.3 copy-start.2
  109.9 1.3 copy-start.3
Sparse Core Ops, SparseCore 0:
  10.4 77.9 all-gather.2
  110.1 89.5 reduce-scatter.1

commit v11 on v10

--- a/solution.py
+++ b/solution.py
@@ -189,20 +189,25 @@
 
 def core_kernel(
     slots, gr_ref, ur_ref, dc_ref, p_hbm, w_hbm, panel_hbm, acts_ref,
-    p_buf, w_buf, out_acc, in_acc, gath, pstage, isem, psem,
+    p_buf, w_buf, out_acc, in_acc, gath, pstage, isem, psem, wsem,
 ):
     f32 = jnp.float32
     bf16 = jnp.bfloat16
     peers, _, rows, chunk = p_buf.shape
     per = chunk // BS
     nt = (((1,), (1,)), ((), ()))
-    cp_w = pltpu.make_async_copy(w_hbm, w_buf, isem.at[0])
-    cp_w.start()
+    def wcopy(s):
+        return pltpu.make_async_copy(w_hbm.at[s], w_buf.at[s], wsem.at[s])
+
+    for part in range(3):
+        wcopy(part * slots).start()
     cp_p = pltpu.make_async_copy(p_hbm, p_buf, isem.at[1])
     cp_p.start()
+    for f in range(1, slots):
+        for part in range(3):
+            wcopy(part * slots + f).start()
     out_acc[...] = jnp.zeros_like(out_acc)
     in_acc[...] = jnp.zeros_like(in_acc)
-    cp_w.wait()
     cp_p.wait()
 
     def col(b):
@@ -217,6 +222,8 @@
             gath[0, :, ks] = block(0, gr_ref[f, k])
             gath[1, :, ks] = block(0, ur_ref[f, k])
             gath[2, :, ks] = block(1, dc_ref[f, k])
+        for part in range(3):
+            wcopy(part * slots + f).wait()
         gw = w_buf[f]
         uw = w_buf[slots + f]
         dw = w_buf[2 * slots + f]
@@ -311,6 +318,7 @@
             pltpu.VMEM(panels.shape, jnp.bfloat16),
             pltpu.SemaphoreType.DMA((2,)),
             pltpu.SemaphoreType.DMA((peers,)),
+            pltpu.SemaphoreType.DMA((tiles.shape[0],)),
         ],
         compiler_params=pltpu.CompilerParams(vmem_limit_bytes=62 * 1024 * 1024),
         cost_estimate=pl.CostEstimate(

time: 211 us -> 214 us (1.014)
  Pallas kernels: 168 us -> 171 us
    pallas_call x1, Pallas kernels: 21.4 us -> 24.7 us  [core(): pl.pallas_call(functools.partial(core_kernel, slots), out_shape=(jax.Shap...]
  transfers between devices with their start and end apart: 2 -> 2, of which waited for: 1 -> 1; matrix products, arithmetic and copies ran while one was open for 1% -> 1% of each run, Pallas kernels for 70% -> 69%
where the time goes in v11:
time: 214 us
  Pallas kernels  171 us (80%)
  waiting for transfers between devices  20.8 us (10%)
  between operations  14.1 us (7%)
  local copies, waits for them, and re-layouts  3.87 us (2%)
  other arithmetic  3.75 us (2%)
    pallas_call x1, Pallas kernels, scatter_rows(): pl.pallas_call(functools.partial(scatter_rows_kernel, n_row), out_shape=j...  79.2 us
    pallas_call x1, Pallas kernels, gather_rows(): pl.pallas_call(functools.partial(gather_rows_kernel, n_row), out_shape=ja...  56.7 us
    pallas_call x1, Pallas kernels, core(): pl.pallas_call(functools.partial(core_kernel, slots), out_shape=(jax.Shap...  24.7 us
    all_gather x1, waiting for transfers between devices, shards(): panels = lax.all_gather(jnp.stack([tokens, out_grad]), 'col', axis=0)  20.7 us
    pallas_call x1, Pallas kernels, core(): pl.pallas_call(functools.partial(tile_kernel, slots), out_shape=jax.Shape...  10.6 us
  transfers between devices with their start and end apart: 2, of which 1 were waited for; matrix products, arithmetic and copies ran while one was open for 1% of the time, Pallas kernels for 69%

profile of v11, /device:TPU:64, one launch (start us, length us, event | category | flops | bytes accessed | tf_op | source)
XLA Modules:
  0.0 213.7 jit_solution(11823178956187101907)
XLA Ops:
  7.2 0.0 all-gather.3.cloned.1.call-start
  7.2 1.9 pad_maximum_fusion
  9.1 0.0 all-gather.3.cloned.1.call-update
  9.2 0.0 reduce-scatter.2.cloned.1.call-start
  9.2 1.8 pad_maximum_fusion.1.w_ref
  11.0 56.7 %shard_map.119.w_hbm = bf16[21,1024,128]{2,1,0:T(8,128)(2,1)} custom-call(bf16[21,64,128]{2,1,0:T(8,128)(2,1)} %pad_maximum_fusion.1.w_ref), custom_call_target="tpu_custom_call" | custom-call | bytes 5505024 | tf_op jit(solution)/shard_map/pallas_call | solution.py:95
  67.7 20.7 %all-gather.3.cloned.1.call-done = bf16[32,256,512]{2,1,0:T(8,128)(2,1)} async-done(((bf16[2,256,512]{2,1,0:T(8,128)(2,1)}), bf16[32,256,512]{2,1,0:T(8,128)(2,1)}) %all-gather.3.cloned.1.call-update) | async-done | bytes 8388624 | tf_op jit(solution)/shard_map/all_gather | solution.py:352
  88.5 24.7 %shard_map.120 = (bf16[16,2,256,512]{3,2,1,0:T(8,128)(2,1)}, bf16[3,7,256,128]{3,2,1,0:T(8,128)(2,1)}) custom-call(s32[7,8]{1,0:T(8,128)} %gr_ref.3, s32[7,8]{1,0:T(8,128)} %ur_ref.3, s32[7,8]{1,0:T(8,128)} %dc_ref.3, bf16[16,2,256,512]{3,2,1,0:T(8,128)(2,1)} %bitcast.6, bf16[21,1024,128]{2,1,0:T(8,128)(2,1)} %shard_map.119.w_hbm), custom_call_target="tpu_custom_call" | custom-call | flops 2818572288 | bytes 22282240 | tf_op jit(solution)/shard_map/pallas_call | solution.py:304
  113.2 0.0 copy-start
  113.2 0.0 copy-start.1
  113.2 0.0 copy-start.2
  113.2 0.0 copy-start.3
  113.2 0.0 reduce-scatter.2.cloned.1.call-update
  113.2 1.3 copy-done
  114.5 0.0 copy-done.1
  114.5 0.0 copy-done.2
  114.5 0.0 copy-done.3
  114.5 10.6 %shard_map.121 = bf16[21,1024,128]{2,1,0:T(8,128)(2,1)S(1)} custom-call(s32[7,8]{1,0:T(8,128)S(1)} %copy-done.1, s32[7,8]{1,0:T(8,128)S(1)} %copy-done.2, s32[7,8]{1,0:T(8,128)S(1)} %copy-done.3, bf16[16,2,256,512]{3,2,1,0:T(8,128)(2,1)} %bitcast.7, bf16[3,7,256,128]{3,2,1,0:T(8,128)(2,1)S(1)} %copy-done), custom_call_target="tpu_custom_call" | custom-call | flops 1409286144 | bytes 13893632 | tf_op jit(solution)/shard_map/pallas_call | solution.py:329
  125.1 79.2 %shard_map.122 = bf16[21,64,128]{2,1,0:T(8,128)(2,1)S(1)} custom-call(bf16[21,8,2,64,128]{4,3,2,1,0:T(8,128)(2,1)S(1)} %bitcast.5), custom_call_target="tpu_custom_call" | custom-call | flops 2752512 | bytes 11010048 | tf_op jit(solution)/shard_map/pallas_call | solution.py:167
  204.3 0.7 fusion.1
  205.1 0.0 reduce-scatter.2.cloned.1.call-done
  205.1 1.9 fusion
Async XLA Ops:
  7.2 81.3 %all-gather.3.cloned.1.call-start = ((), (), s32[]{:S(2)}) async-start(), calls=%async_computation.2 | async-start | bytes 8912896 | tf_op jit(solution)/shard_map/all_gather | solution.py:352
  9.2 195.9 %reduce-scatter.2.cloned.1.call-start = ((), (), s32[]{:S(2)}) async-start(), calls=%async_computation.1 | async-start | bytes 8912896 | tf_op jit(solution)/shard_map/reduce_scatter | solution.py:358
  113.2 1.3 copy-start
  113.2 1.3 copy-start.1
  113.2 1.3 copy-start.2
  113.2 1.3 copy-start.3
Sparse Core Ops, SparseCore 0:
  10.4 77.9 all-gather.2
  113.4 89.7 reduce-scatter.1

commit v12 on v10

--- a/solution.py
+++ b/solution.py
@@ -189,21 +189,25 @@
 
 def core_kernel(
     slots, gr_ref, ur_ref, dc_ref, p_hbm, w_hbm, panel_hbm, acts_ref,
-    p_buf, w_buf, out_acc, in_acc, gath, pstage, isem, psem,
+    p_buf, w_buf, out_acc, in_acc, gath, pstage, isem, psem, wsem, psem_in,
 ):
     f32 = jnp.float32
     bf16 = jnp.bfloat16
     peers, _, rows, chunk = p_buf.shape
     per = chunk // BS
     nt = (((1,), (1,)), ((), ()))
-    cp_w = pltpu.make_async_copy(w_hbm, w_buf, isem.at[0])
-    cp_w.start()
-    cp_p = pltpu.make_async_copy(p_hbm, p_buf, isem.at[1])
-    cp_p.start()
+    copies = []
+    for part in range(3):
+        ws = pl.ds(part * slots, slots)
+        copies.append(pltpu.make_async_copy(w_hbm.at[ws], w_buf.at[ws], wsem.at[part]))
+    for j in range(peers):
+        copies.append(pltpu.make_async_copy(p_hbm.at[j], p_buf.at[j], psem_in.at[j]))
+    for cp in copies:
+        cp.start()
     out_acc[...] = jnp.zeros_like(out_acc)
     in_acc[...] = jnp.zeros_like(in_acc)
-    cp_w.wait()
-    cp_p.wait()
+    for cp in copies:
+        cp.wait()
 
     def col(b):
         return pl.ds(pl.multiple_of(b * BS, BS), BS)
@@ -311,6 +315,8 @@
             pltpu.VMEM(panels.shape, jnp.bfloat16),
             pltpu.SemaphoreType.DMA((2,)),
             pltpu.SemaphoreType.DMA((peers,)),
+            pltpu.SemaphoreType.DMA((3,)),
+            pltpu.SemaphoreType.DMA((peers,)),
         ],
         compiler_params=pltpu.CompilerParams(vmem_limit_bytes=62 * 1024 * 1024),
         cost_estimate=pl.CostEstimate(

time: 211 us -> 211 us (level)
  no operation moved by 1% of the time
where the time goes in v12:
time: 211 us
  Pallas kernels  168 us (80%)
  waiting for transfers between devices  20.8 us (10%)
  between operations  14.1 us (7%)
  local copies, waits for them, and re-layouts  3.87 us (2%)
  other arithmetic  3.75 us (2%)
    pallas_call x1, Pallas kernels, scatter_rows(): pl.pallas_call(functools.partial(scatter_rows_kernel, n_row), out_shape=j...  79.2 us
    pallas_call x1, Pallas kernels, gather_rows(): pl.pallas_call(functools.partial(gather_rows_kernel, n_row), out_shape=ja...  56.7 us
    pallas_call x1, Pallas kernels, core(): pl.pallas_call(functools.partial(core_kernel, slots), out_shape=(jax.Shap...  21.5 us
    all_gather x1, waiting for transfers between devices, shards(): panels = lax.all_gather(jnp.stack([tokens, out_grad]), 'col', axis=0)  20.7 us
    pallas_call x1, Pallas kernels, core(): pl.pallas_call(functools.partial(tile_kernel, slots), out_shape=jax.Shape...  10.6 us
  transfers between devices with their start and end apart: 2, of which 1 were waited for; matrix products, arithmetic and copies ran while one was open for 1% of the time, Pallas kernels for 70%

profile of v12, /device:TPU:64, one launch (start us, length us, event | category | flops | bytes accessed | tf_op | source)
XLA Modules:
  0.0 210.6 jit_solution(17180803356124571965)
XLA Ops:
  7.2 0.0 all-gather.3.cloned.1.call-start
  7.2 1.9 pad_maximum_fusion
  9.1 0.0 all-gather.3.cloned.1.call-update
  9.2 0.0 reduce-scatter.2.cloned.1.call-start
  9.2 1.8 pad_maximum_fusion.1.w_ref
  11.0 56.7 %shard_map.119.w_hbm = bf16[21,1024,128]{2,1,0:T(8,128)(2,1)} custom-call(bf16[21,64,128]{2,1,0:T(8,128)(2,1)} %pad_maximum_fusion.1.w_ref), custom_call_target="tpu_custom_call" | custom-call | bytes 5505024 | tf_op jit(solution)/shard_map/pallas_call | solution.py:95
  67.7 20.7 %all-gather.3.cloned.1.call-done = bf16[32,256,512]{2,1,0:T(8,128)(2,1)} async-done(((bf16[2,256,512]{2,1,0:T(8,128)(2,1)}), bf16[32,256,512]{2,1,0:T(8,128)(2,1)}) %all-gather.3.cloned.1.call-update) | async-done | bytes 8388624 | tf_op jit(solution)/shard_map/all_gather | solution.py:350
  88.5 21.5 %shard_map.120 = (bf16[16,2,256,512]{3,2,1,0:T(8,128)(2,1)}, bf16[3,7,256,128]{3,2,1,0:T(8,128)(2,1)}) custom-call(s32[7,8]{1,0:T(8,128)} %gr_ref.3, s32[7,8]{1,0:T(8,128)} %ur_ref.3, s32[7,8]{1,0:T(8,128)} %dc_ref.3, bf16[16,2,256,512]{3,2,1,0:T(8,128)(2,1)} %bitcast.6, bf16[21,1024,128]{2,1,0:T(8,128)(2,1)} %shard_map.119.w_hbm), custom_call_target="tpu_custom_call" | custom-call | flops 2818572288 | bytes 22282240 | tf_op jit(solution)/shard_map/pallas_call | solution.py:301
  110.0 0.0 copy-start
  110.0 0.0 copy-start.1
  110.0 0.0 copy-start.2
  110.1 0.0 copy-start.3
  110.1 0.0 reduce-scatter.2.cloned.1.call-update
  110.1 1.3 copy-done
  111.4 0.0 copy-done.1
  111.4 0.0 copy-done.2
  111.4 0.0 copy-done.3
  111.4 10.6 %shard_map.121 = bf16[21,1024,128]{2,1,0:T(8,128)(2,1)S(1)} custom-call(s32[7,8]{1,0:T(8,128)S(1)} %copy-done.1, s32[7,8]{1,0:T(8,128)S(1)} %copy-done.2, s32[7,8]{1,0:T(8,128)S(1)} %copy-done.3, bf16[16,2,256,512]{3,2,1,0:T(8,128)(2,1)} %bitcast.7, bf16[3,7,256,128]{3,2,1,0:T(8,128)(2,1)S(1)} %copy-done), custom_call_target="tpu_custom_call" | custom-call | flops 1409286144 | bytes 13893632 | tf_op jit(solution)/shard_map/pallas_call | solution.py:327
  122.0 79.2 %shard_map.122 = bf16[21,64,128]{2,1,0:T(8,128)(2,1)S(1)} custom-call(bf16[21,8,2,64,128]{4,3,2,1,0:T(8,128)(2,1)S(1)} %bitcast.5), custom_call_target="tpu_custom_call" | custom-call | flops 2752512 | bytes 11010048 | tf_op jit(solution)/shard_map/pallas_call | solution.py:167
  201.2 0.7 fusion.1
  201.9 0.0 reduce-scatter.2.cloned.1.call-done
  201.9 1.9 fusion
Async XLA Ops:
  7.2 81.3 %all-gather.3.cloned.1.call-start = ((), (), s32[]{:S(2)}) async-start(), calls=%async_computation.2 | async-start | bytes 8912896 | tf_op jit(solution)/shard_map/all_gather | solution.py:350
  9.2 192.8 %reduce-scatter.2.cloned.1.call-start = ((), (), s32[]{:S(2)}) async-start(), calls=%async_computation.1 | async-start | bytes 8912896 | tf_op jit(solution)/shard_map/reduce_scatter | solution.py:356
  110.0 1.3 copy-start
  110.0 1.3 copy-start.1
  110.0 1.3 copy-start.2
  110.1 1.3 copy-start.3
Sparse Core Ops, SparseCore 0:
  10.4 77.9 all-gather.2
  110.2 89.4 reduce-scatter.1

commit v13 on v10

--- a/solution.py
+++ b/solution.py
@@ -111,7 +111,9 @@
     )(w)
 
 
-def scatter_rows_kernel(n_row, x_ref, out_ref, part_buf, send_buf, recv_buf, psend, precv, rsend, rrecv):
+def scatter_rows_kernel(
+    n_row, x_ref, out_ref, own_buf, part_buf, send_buf, recv_buf, osem, psend, precv, rsend, rrecv
+):
     me = lax.axis_index("row")
     n_chip = n_row // 2
     z = me // 2
@@ -122,6 +124,8 @@
     prv = ((z - step_dir + n_chip) % n_chip) * 2 + c
     f32 = jnp.float32
 
+    own = pltpu.make_async_copy(x_ref.at[:, :, c], own_buf, osem)
+    own.start()
     barrier = pltpu.get_barrier_semaphore()
     for peer in (partner, nxt, prv):
         pl.semaphore_signal(barrier, inc=1, device_id={"row": peer}, device_id_type=MESH)
@@ -133,9 +137,10 @@
     )
     swap.start()
     swap.wait_recv()
+    own.wait()
 
     def chip_part(q):
-        return x_ref[:, q, c].astype(f32) + part_buf[:, q].astype(f32)
+        return own_buf[:, q].astype(f32) + part_buf[:, q].astype(f32)
 
     sends = []
     for s in range(1, n_chip):
@@ -167,12 +172,14 @@
     return pl.pallas_call(
         functools.partial(scatter_rows_kernel, n_row),
         out_shape=jax.ShapeDtypeStruct((slots, half, width), x.dtype),
-        in_specs=[vmem],
+        in_specs=[pl.BlockSpec(memory_space=pl.ANY)],
         out_specs=vmem,
         scratch_shapes=[
             pltpu.VMEM((slots, n_chip, half, width), x.dtype),
+            pltpu.VMEM((slots, n_chip, half, width), x.dtype),
             pltpu.VMEM((n_chip - 1, slots, half, width), jnp.float32),
             pltpu.VMEM((n_chip - 1, slots, half, width), jnp.float32),
+            pltpu.SemaphoreType.DMA(()),
             pltpu.SemaphoreType.DMA(()),
             pltpu.SemaphoreType.DMA(()),
             pltpu.SemaphoreType.DMA((n_chip - 1,)),

time: 211 us -> 211 us (level)
  no operation moved by 1% of the time
where the time goes in v13:
time: 211 us
  Pallas kernels  168 us (80%)
  waiting for transfers between devices  20.8 us (10%)
  between operations  14.1 us (7%)
  local copies, waits for them, and re-layouts  3.87 us (2%)
  other arithmetic  3.75 us (2%)
    pallas_call x1, Pallas kernels, scatter_rows(): pl.pallas_call(functools.partial(scatter_rows_kernel, n_row), out_shape=j...  79.7 us
    pallas_call x1, Pallas kernels, gather_rows(): pl.pallas_call(functools.partial(gather_rows_kernel, n_row), out_shape=ja...  56.7 us
    pallas_call x1, Pallas kernels, core(): pl.pallas_call(functools.partial(core_kernel, slots), out_shape=(jax.Shap...  21.4 us
    all_gather x1, waiting for transfers between devices, shards(): panels = lax.all_gather(jnp.stack([tokens, out_grad]), 'col', axis=0)  20.7 us
    pallas_call x1, Pallas kernels, core(): pl.pallas_call(functools.partial(tile_kernel, slots), out_shape=jax.Shape...  10.6 us
  transfers between devices with their start and end apart: 2, of which 1 were waited for; matrix products, arithmetic and copies ran while one was open for 1% of the time, Pallas kernels for 70%

profile of v13, /device:TPU:64, one launch (start us, length us, event | category | flops | bytes accessed | tf_op | source)
XLA Modules:
  0.0 211.0 jit_solution(12701506766408813466)
XLA Ops:
  7.2 0.0 all-gather.3.cloned.1.call-start
  7.2 1.9 pad_maximum_fusion
  9.1 0.0 all-gather.3.cloned.1.call-update
  9.2 0.0 reduce-scatter.2.cloned.1.call-start
  9.2 1.8 pad_maximum_fusion.1.w_ref
  11.0 56.7 %shard_map.119.w_hbm = bf16[21,1024,128]{2,1,0:T(8,128)(2,1)} custom-call(bf16[21,64,128]{2,1,0:T(8,128)(2,1)} %pad_maximum_fusion.1.w_ref), custom_call_target="tpu_custom_call" | custom-call | bytes 5505024 | tf_op jit(solution)/shard_map/pallas_call | solution.py:95
  67.7 20.7 %all-gather.3.cloned.1.call-done = bf16[32,256,512]{2,1,0:T(8,128)(2,1)} async-done(((bf16[2,256,512]{2,1,0:T(8,128)(2,1)}), bf16[32,256,512]{2,1,0:T(8,128)(2,1)}) %all-gather.3.cloned.1.call-update) | async-done | bytes 8388624 | tf_op jit(solution)/shard_map/all_gather | solution.py:351
  88.5 21.4 %shard_map.120 = (bf16[16,2,256,512]{3,2,1,0:T(8,128)(2,1)}, bf16[3,7,256,128]{3,2,1,0:T(8,128)(2,1)}) custom-call(s32[7,8]{1,0:T(8,128)} %gr_ref.3, s32[7,8]{1,0:T(8,128)} %ur_ref.3, s32[7,8]{1,0:T(8,128)} %dc_ref.3, bf16[16,2,256,512]{3,2,1,0:T(8,128)(2,1)} %bitcast.6, bf16[21,1024,128]{2,1,0:T(8,128)(2,1)} %shard_map.119.w_hbm), custom_call_target="tpu_custom_call" | custom-call | flops 2818572288 | bytes 22282240 | tf_op jit(solution)/shard_map/pallas_call | solution.py:304
  109.9 0.0 copy-start
  109.9 0.0 copy-start.1
  109.9 0.0 copy-start.2
  109.9 0.0 copy-start.3
  109.9 0.0 reduce-scatter.2.cloned.1.call-update
  110.0 1.3 copy-done
  111.2 0.0 copy-done.1
  111.2 0.0 copy-done.2
  111.2 0.0 copy-done.3
  111.2 10.6 %shard_map.121 = bf16[21,1024,128]{2,1,0:T(8,128)(2,1)S(1)} custom-call(s32[7,8]{1,0:T(8,128)S(1)} %copy-done.1, s32[7,8]{1,0:T(8,128)S(1)} %copy-done.2, s32[7,8]{1,0:T(8,128)S(1)} %copy-done.3, bf16[16,2,256,512]{3,2,1,0:T(8,128)(2,1)} %bitcast.7, bf16[3,7,256,128]{3,2,1,0:T(8,128)(2,1)S(1)} %copy-done), custom_call_target="tpu_custom_call" | custom-call | flops 1409286144 | bytes 13893632 | tf_op jit(solution)/shard_map/pallas_call | solution.py:328
  121.9 79.7 %shard_map.122 = bf16[21,64,128]{2,1,0:T(8,128)(2,1)S(1)} custom-call(bf16[21,8,2,64,128]{4,3,2,1,0:T(8,128)(2,1)S(1)} %bitcast.5), custom_call_target="tpu_custom_call" | custom-call | flops 2752512 | bytes 11010048 | tf_op jit(solution)/shard_map/pallas_call | solution.py:172
  201.6 0.7 fusion.1
  202.3 0.0 reduce-scatter.2.cloned.1.call-done
  202.3 1.9 fusion
Async XLA Ops:
  7.2 81.3 %all-gather.3.cloned.1.call-start = ((), (), s32[]{:S(2)}) async-start(), calls=%async_computation.2 | async-start | bytes 8912896 | tf_op jit(solution)/shard_map/all_gather | solution.py:351
  9.2 193.1 %reduce-scatter.2.cloned.1.call-start = ((), (), s32[]{:S(2)}) async-start(), calls=%async_computation.1 | async-start | bytes 8912896 | tf_op jit(solution)/shard_map/reduce_scatter | solution.py:357
  109.9 1.3 copy-start
  109.9 1.3 copy-start.1
  109.9 1.3 copy-start.2
  109.9 1.3 copy-start.3
Sparse Core Ops, SparseCore 0:
  10.4 77.9 all-gather.2
  110.1 89.5 reduce-scatter.1
